TPU v7x, 32 devices: a whole 2x2x4 slice. The times are simulated.
32 devices in a mesh: brick: 8 (over z, y), ch: 4 (over x, core).
Axes of the slice: x: 2, y: 2, z: 4, core: 2. Of those that a mesh axis runs over, the one named last changes fastest.
Arguments:
- features: bfloat16 [256, 1024], P('ch', 'brick'), may hold values from -6 to 6
- owner_map: int32 [1024, 1], P('brick'), may hold values from 0 to 7; in each aligned block of 128 rows (0 to 127, 128 to 255, ...) at most 32 rows name the same one
- kernel_map: int32 [27, 2048], P(None, 'brick'), may hold values from 0 to 320, as said below
- send_lists: int32 [2, 256], P(None, 'brick'), may hold values from 0 to 255
- drop_first: int32 [256, 2048], P('ch', 'brick'), may hold values 0 or 1
- drop_second: int32 [256, 2048], P('ch', 'brick'), may hold values 0 or 1
- weight_first: bfloat16 [27, 256, 256], P(None, 'ch'), may hold values from -0.15625 to 0.15625
- weight_second: bfloat16 [27, 256, 256], P(None, 'ch'), may hold values from -0.15625 to 0.15625
- cotangent: bfloat16 [256, 2048], P('ch', 'brick'), may hold values from -6 to 6
Outputs:
- block_out: bfloat16 [256, 2048], P('ch', 'brick')
- grad_features: bfloat16 [256, 1024], P('ch', 'brick')
- grad_weight_first: bfloat16 [27, 256, 256], P(None, 'ch')
- grad_weight_second: bfloat16 [27, 256, 256], P(None, 'ch')
Inputs may be any that keep to these rules, and one draw needn't show every extreme that they name: `owner_map`: among the rows of one scan group, at most 32 are owned by the same brick. `kernel_map`: column 320 means that the neighbour is absent; in the middle offset row, slot i of every brick names column 32 + i.
All inputs are finite; a program needn't handle non-finite values. No bound on the sum of `drop_first` or of `drop_second` on one device may be relied on, other than what follows from the above.
Results may differ from a plain program's by a relative error of at most 0.0064.
Values may be sent and summed in bfloat16 or wider, within the bound.
No kernel may reach another device: no remote copies, remote signals or barrier semaphores. Data moves between devices by JAX's collectives and lax.ppermute only.
A program may use at most 64 MiB of HBM per device.

v0:
```python
import jax
import jax.numpy as jnp
from jax import lax
from jax.sharding import PartitionSpec as P

KEEP_RATE = 0.9


def with_halo(block, sides, width):
    for axis, dim in sides:
        count = lax.axis_size(axis)
        forward = [(i, i + 1) for i in range(count - 1)]
        backward = [(target, source) for source, target in forward]
        low = lax.ppermute(
            lax.slice_in_dim(block, block.shape[dim] - width, None, axis=dim), axis, forward
        )
        high = lax.ppermute(lax.slice_in_dim(block, 0, width, axis=dim), axis, backward)
        block = jnp.concatenate([low, block, high], axis=dim)
    return block


def slope_silu(value):
    sig = jax.nn.sigmoid(value)
    return sig * (1.0 + value * (1.0 - sig))


def spread(field, send_lists):
    rim_width = send_lists.shape[1]
    outgoing = jnp.concatenate(
        [jnp.take(field, send_lists[0], axis=1), jnp.take(field, send_lists[1], axis=1)], axis=1
    )
    padded = with_halo(outgoing, (("brick", 1),), rim_width)
    return jnp.concatenate([padded[:, :rim_width], field, padded[:, 3 * rim_width :]], axis=1)


def convolve(extended, kernel_map, weight):
    gathered = jnp.take(extended, kernel_map, axis=1, mode="fill", fill_value=0)
    return (
        lax.psum_scatter(
            jnp.einsum("ckr,kco->or", gathered, weight, preferred_element_type=jnp.float32),
            "ch",
            scatter_dimension=0,
            tiled=True,
        ),
        gathered,
    )


def adjoint(gathered, kernel_map, grad_local, weight, extent):
    gathered_grad = lax.all_gather(grad_local, "ch", axis=0, tiled=True)
    weight_grad = jnp.einsum(
        "ckr,or->kco", gathered, gathered_grad, preferred_element_type=jnp.float32
    )
    pushed = jnp.einsum("kco,or->ckr", weight, gathered_grad, preferred_element_type=jnp.float32)
    returned = (
        jnp.zeros((pushed.shape[0], extent), jnp.float32).at[:, kernel_map].add(pushed, mode="drop")
    )
    return (weight_grad, returned)


def fold_back(returned, send_lists, slot_count):
    rim_width = send_lists.shape[1]
    borders = jnp.concatenate(
        [returned[:, :rim_width], returned[:, rim_width + slot_count :]], axis=1
    )
    padded = with_halo(borders, (("brick", 1),), rim_width)
    interior = returned[:, rim_width : rim_width + slot_count]
    interior = interior.at[:, send_lists[0]].add(padded[:, :rim_width])
    return interior.at[:, send_lists[1]].add(padded[:, 3 * rim_width :])


def local(
    features,
    owner_map,
    kernel_map,
    send_lists,
    drop_first,
    drop_second,
    weight_first,
    weight_second,
    cotangent,
):
    bricks = lax.axis_size("brick")
    channels = features.shape[0]
    slot_count = 2 * features.shape[1]
    capacity = slot_count // bricks
    targets = owner_map[:, 0]
    matches = (targets[:, None] == jnp.arange(bricks, dtype=jnp.int32)[None, :]).astype(jnp.int32)
    running = jnp.cumsum(matches, axis=0)
    ordinal = jnp.sum((running - 1) * matches, axis=1)
    columns = targets * capacity + ordinal
    outgoing = jnp.zeros((channels, slot_count), features.dtype).at[:, columns].set(features)
    tallies = jnp.sum(matches, axis=0)[None, :].astype(jnp.bfloat16)
    arrived, arrived_tallies = (
        lax.all_to_all(
            outgoing.reshape(channels, bricks, capacity),
            "brick",
            split_axis=1,
            concat_axis=1,
            tiled=True,
        ),
        lax.all_to_all(tallies, "brick", split_axis=1, concat_axis=1, tiled=True),
    )
    voxels = arrived.reshape(channels, slot_count)
    occupied = (
        jnp.arange(capacity, dtype=jnp.int32)[None, :]
        < arrived_tallies[0].astype(jnp.int32)[:, None]
    )
    occupied = occupied.reshape(slot_count).astype(jnp.float32)
    keep_first = occupied[None, :] * drop_first.astype(jnp.float32) / KEEP_RATE
    keep_second = occupied[None, :] * drop_second.astype(jnp.float32) / KEEP_RATE
    extended_voxels = spread(voxels, send_lists)
    extent = extended_voxels.shape[1]
    conv_first, gathered_voxels = convolve(extended_voxels, kernel_map, weight_first)
    hidden = (jax.nn.silu(conv_first) * keep_first).astype(jnp.bfloat16)
    extended_hidden = spread(hidden, send_lists)
    conv_second, gathered_hidden = convolve(extended_hidden, kernel_map, weight_second)
    summed = voxels.astype(jnp.float32) + keep_second * conv_second
    block_out = jax.nn.silu(summed).astype(jnp.bfloat16)
    grad_pre = cotangent.astype(jnp.float32) * slope_silu(summed)
    grad_second = (grad_pre * keep_second).astype(jnp.bfloat16)
    weight_grad_second, returned_second = adjoint(
        gathered_hidden, kernel_map, grad_second, weight_second, extent
    )
    grad_hidden = fold_back(returned_second, send_lists, slot_count)
    grad_first = (grad_hidden * keep_first * slope_silu(conv_first)).astype(jnp.bfloat16)
    weight_grad_first, returned_first = adjoint(
        gathered_voxels, kernel_map, grad_first, weight_first, extent
    )
    weight_grad_first, weight_grad_second = lax.psum(
        (weight_grad_first, weight_grad_second), "brick"
    )
    grad_voxels = (grad_pre + fold_back(returned_first, send_lists, slot_count)).astype(
        jnp.bfloat16
    )
    homeward = lax.all_to_all(
        grad_voxels.reshape(channels, bricks, capacity),
        "brick",
        split_axis=1,
        concat_axis=1,
        tiled=True,
    )
    grad_features = jnp.take(homeward.reshape(channels, slot_count), columns, axis=1)
    factor = float(bricks * slot_count) ** (-0.5)
    return (
        block_out,
        grad_features,
        (weight_grad_first * factor).astype(jnp.bfloat16),
        (weight_grad_second * factor).astype(jnp.bfloat16),
    )


def solution(mesh):
    return jax.shard_map(
        local,
        mesh=mesh,
        in_specs=(
            P("ch", "brick"),
            P("brick", None),
            P(None, "brick"),
            P(None, "brick"),
            P("ch", "brick"),
            P("ch", "brick"),
            P(None, "ch", None),
            P(None, "ch", None),
            P("ch", "brick"),
        ),
        out_specs=(P("ch", "brick"), P("ch", "brick"), P(None, "ch", None), P(None, "ch", None)),
        check_vma=False,
    )
```

profile of v0, /device:TPU:0, one launch (start us, length us, event | category | flops | bytes accessed | tf_op | source)
XLA Modules:
  0.0 336.1 jit_solution(5899775160566598532)
XLA Ops:
  8.2 1.4 fusion.19
  13.3 7.3 %all-to-all-start = ((bf16[8,2,1024]{2,1,0:T(2,128)(2,1)}), bf16[8,2,1024]{2,1,0:T(2,128)(2,1)S(1)}, u32[]{:S(2)}, u32[]{:S(2)}) async-start(bf16[8,2,1024]{2,1,0:T(2,128)(2,1)} %reshape.297), calls=%async_computation | async-start | bytes 65536 | tf_op jit(solution)/shard_map/all_to_all | solution.py:95
  23.1 4.3 %all-to-all-done = bf16[8,2,1024]{2,1,0:T(2,128)(2,1)S(1)} async-done(((bf16[8,2,1024]{2,1,0:T(2,128)(2,1)}), bf16[8,2,1024]{2,1,0:T(2,128)(2,1)S(1)}, u32[]{:S(2)}, u32[]{:S(2)}) %all-to-all-start) | async-done | bytes 32800 | tf_op jit(solution)/shard_map/all_to_all | solution.py:95
  28.1 2.4 collective-permute-start
  32.5 4.2 %collective-permute-done.1 = bf16[64,32]{0,1:T(8,128)(2,1)S(1)} collective-permute-done((bf16[64,32]{0,1:T(8,128)(2,1)S(1)}, bf16[64,32]{0,1:T(8,128)(2,1)S(1)}, u32[]{:S(2)}, u32[]{:S(2)}) %collective-permute-start.1) | collective-permute-done | bytes 4128 | tf_op jit(solution)/shard_map/ppermute | solution.py:17
  36.7 13.0 %gather_fusion.3 = bf16[6912,64]{1,0:T(8,128)(2,1)S(1)} fusion(bf16[64,320]{0,1:T(8,128)(2,1)S(1)} %pad_maximum_fusion, s32[7168]{0:T(1024)S(1)} %pad_clamp_fusion), kind=kCustom, calls=%fused_computation.1.clone | custom fusion | bytes 1797120 | tf_op jit(solution)/shard_map/jit(_take)/gather | solution.py:37
  50.7 2.0 convolution_bitcast_fusion.5
  53.8 10.0 %all_to_all.16 = bf16[1,8,1]{2,0,1:T(2,128)(2,1)S(1)} all-to-all(bf16[1,8,1]{2,0,1:T(2,128)(2,1)S(1)} %copy.100), channel_id=1, replica_groups=mesh['brick'=8,'ch'=4] {'brick'}, dimensions={1} | all-to-all | bytes 32 | tf_op jit(solution)/shard_map/all_to_all | solution.py:102
  64.2 8.8 %reduce-scatter.7.cloned.1.call-done = f32[64,256]{1,0:T(8,128)} async-done(((f32[256,256]{1,0:T(8,128)}), f32[64,256]{1,0:T(8,128)}) %reduce-scatter.7.cloned.1.call-update) | async-done | bytes 65552 | tf_op jit(solution)/shard_map/reduce_scatter | solution.py:39
  75.4 3.4 %collective-permute-start.2 = (bf16[64,32]{1,0:T(8,128)(2,1)S(1)}, bf16[64,32]{1,0:T(8,128)(2,1)S(1)}, u32[]{:S(2)}, u32[]{:S(2)}) collective-permute-start(bf16[64,32]{1,0:T(8,128)(2,1)S(1)} %select_bitcast_fusion.2), channel_id=1, source_target_pairs={{0,4},{4,8},{8,12},{12,16},{16,20},{20,24},{24,28},{1,5},{5,9},{9,... | collective-permute-start | bytes 12296 | tf_op jit(solution)/shard_map/ppermute | solution.py:14
  78.9 1.3 collective-permute-start.3
  80.2 4.3 %collective-permute-done.3 = bf16[64,32]{1,0:T(8,128)(2,1)S(1)} collective-permute-done((bf16[64,32]{1,0:T(8,128)(2,1)S(1)}, bf16[64,32]{1,0:T(8,128)(2,1)S(1)}, u32[]{:S(2)}, u32[]{:S(2)}) %collective-permute-start.3) | collective-permute-done | bytes 4128 | tf_op jit(solution)/shard_map/ppermute | solution.py:17
  84.8 13.0 %gather_fusion.6 = bf16[6912,64]{1,0:T(8,128)(2,1)S(1)} fusion(bf16[64,320]{0,1:T(8,128)(2,1)S(1)} %copy.108, s32[7168]{0:T(1024)S(1)} %copy-done.7), kind=kCustom, calls=%fused_computation.5.clone | custom fusion | bytes 1797120 | tf_op jit(solution)/shard_map/jit(_take)/gather | solution.py:37
  100.8 19.5 %reduce-scatter.9.cloned.1.call-done = f32[64,256]{1,0:T(8,128)} async-done(((f32[256,256]{1,0:T(8,128)}), f32[64,256]{1,0:T(8,128)}) %reduce-scatter.9.cloned.1.call-update) | async-done | bytes 65552 | tf_op jit(solution)/shard_map/reduce_scatter | solution.py:39
  121.1 5.4 %all_gather.6 = bf16[256,256]{1,0:T(8,128)(2,1)S(1)} all-gather(bf16[64,256]{1,0:T(8,128)(2,1)S(1)} %multiply_convert_fusion.3), channel_id=1, replica_groups=mesh['brick'=8,'ch'=4] {'ch'}, dimensions={0}, use_global_device_ids=true | all-gather | bytes 163840 | tf_op jit(solution)/shard_map/all_gather | solution.py:50
  127.6 2.5 copy.120
  130.1 39.1 %scatter_custom_fusion.1 = f32[64,320]{0,1:T(8,128)S(1)} fusion(s32[6912]{0:T(1024)} %copy-done.18, f32[6912,64]{1,0:T(8,128)} %bitcast.105, f32[]{:T(128)} %constant.44.clone.1), kind=kCustom, calls=%fused_computation.40 | custom fusion | flops 442368 | bytes 82432 | tf_op jit(solution)/shard_map/scatter-add | solution.py:56
  169.2 3.4 %collective-permute-start.4 = (f32[64,32]{0,1:T(8,128)S(1)}, f32[64,32]{0,1:T(8,128)S(1)}, u32[]{:S(2)}, u32[]{:S(2)}) collective-permute-start(f32[64,32]{0,1:T(8,128)S(1)} %get-tuple-element.45), channel_id=1, source_target_pairs={{0,4},{4,8},{8,12},{12,16},{16,20},{20,24},{24,28},{1,5},{5,9},{9,... | collective-permute-start | bytes 24584 | tf_op jit(solution)/shard_map/ppermute | solution.py:14
  172.6 1.4 collective-permute-start.5
  174.0 2.6 convolution_bitcast_fusion
  179.3 5.6 %all_gather.7 = bf16[256,256]{1,0:T(8,128)(2,1)S(1)} all-gather(bf16[64,256]{1,0:T(8,128)(2,1)S(1)} %multiply_convert_fusion.2), channel_id=1, replica_groups=mesh['brick'=8,'ch'=4] {'ch'}, dimensions={0}, use_global_device_ids=true | all-gather | bytes 163840 | tf_op jit(solution)/shard_map/all_gather | solution.py:50
  184.9 1.7 convolution_bitcast_fusion.1
  186.6 1.6 convolution_bitcast_fusion.2
  188.2 2.5 copy.121
  190.7 39.1 %scatter_custom_fusion.4 = f32[64,320]{0,1:T(8,128)S(1)} fusion(s32[6912]{0:T(1024)} %copy-done.18, f32[6912,64]{1,0:T(8,128)} %bitcast.104, f32[]{:T(128)} %constant.44.clone.1), kind=kCustom, calls=%fused_computation.38 | custom fusion | flops 442368 | bytes 82432 | tf_op jit(solution)/shard_map/scatter-add | solution.py:56
  229.9 4.3 %collective-permute-start.6 = (f32[64,32]{0,1:T(8,128)S(1)}, f32[64,32]{0,1:T(8,128)S(1)}, u32[]{:S(2)}, u32[]{:S(2)}) collective-permute-start(f32[64,32]{0,1:T(8,128)S(1)} %get-tuple-element.43), channel_id=1, source_target_pairs={{0,4},{4,8},{8,12},{12,16},{16,20},{20,24},{24,28},{1,5},{5,9},{9,... | collective-permute-start | bytes 24584 | tf_op jit(solution)/shard_map/ppermute | solution.py:14
  234.2 1.3 collective-permute-start.7
  237.2 2.6 collective-permute-done.7
  241.4 6.0 %all-to-all-start.2 = ((bf16[8,2,1024]{2,1,0:T(2,128)(2,1)}), bf16[8,2,1024]{2,1,0:T(2,128)(2,1)S(1)}, u32[]{:S(2)}, u32[]{:S(2)}) async-start(bf16[8,2,1024]{2,1,0:T(2,128)(2,1)} %reshape.299), calls=%async_computation.2 | async-start | bytes 65536 | tf_op jit(solution)/shard_map/all_to_all | solution.py:136
  247.4 7.1 %all-to-all-done.2 = bf16[8,2,1024]{2,1,0:T(2,128)(2,1)S(1)} async-done(((bf16[8,2,1024]{2,1,0:T(2,128)(2,1)}), bf16[8,2,1024]{2,1,0:T(2,128)(2,1)S(1)}, u32[]{:S(2)}, u32[]{:S(2)}) %all-to-all-start.2) | async-done | bytes 32800 | tf_op jit(solution)/shard_map/all_to_all | solution.py:136
  256.1 69.7 %all-reduce.3.cloned.1.call-done = (f32[27,64,256]{2,1,0:T(8,128)}, f32[27,64,256]{2,1,0:T(8,128)}) async-done(((f32[27,64,256]{2,1,0:T(8,128)}, f32[27,64,256]{2,1,0:T(8,128)}), (f32[27,64,256]{2,1,0:T(8,128)}, f32[27,64,256]{2,1,0:T(8,128)})) %all-reduce.3.cloned.1.call-update) | async-done | bytes 3538960 | tf_op jit(solution)/shard_map/psum | solution.py:130
  325.9 3.7 %multiply_convert_fusion = (bf16[27,64,256]{2,1,0:T(8,128)(2,1)}, bf16[27,64,256]{2,1,0:T(8,128)(2,1)}) fusion(f32[27,64,256]{2,1,0:T(8,128)} %get-tuple-element.33, f32[27,64,256]{2,1,0:T(8,128)} %get-tuple-element.32), kind=kLoop, calls=%fused_computation.14 | loop fusion | flops 1769472 | bytes 5308416 | tf_op jit(solution)/shard_map/convert_element_type | solution.py:149
  (133 shorter events, 27.3 us)
Async XLA Ops:
  7.2 91.5 %copy-start = (bf16[27,64,256]{2,1,0:T(8,128)(2,1)S(1)}, bf16[27,64,256]{2,1,0:T(8,128)(2,1)}, u32[]{:S(2)}) copy-start(bf16[27,64,256]{2,1,0:T(8,128)(2,1)} %param.20) | copy-start | bytes 2654212
  13.3 14.0 %all-to-all-start = ((bf16[8,2,1024]{2,1,0:T(2,128)(2,1)}), bf16[8,2,1024]{2,1,0:T(2,128)(2,1)S(1)}, u32[]{:S(2)}, u32[]{:S(2)}) async-start(bf16[8,2,1024]{2,1,0:T(2,128)(2,1)} %reshape.297), calls=%async_computation | async-start | bytes 65536 | tf_op jit(solution)/shard_map/all_to_all | solution.py:95
  20.6 52.3 %reduce-scatter.7.cloned.1.call-start = ((), (), s32[]{:S(2)}) async-start(), calls=%async_computation.5 | async-start | bytes 327680 | tf_op jit(solution)/shard_map/reduce_scatter | solution.py:39
  23.0 13.7 %copy-start.20 = (pred[32]{0:T(512)(128)(4,1)}, pred[32]{0:T(512)(128)(4,1)S(1)}, u32[]{:S(2)}) copy-start(pred[32]{0:T(512)(128)(4,1)S(1)} %get-tuple-element.48) | copy-start | bytes 100
  23.0 13.7 %copy-start.22 = (pred[32]{0:T(512)(128)(4,1)}, pred[32]{0:T(512)(128)(4,1)S(1)}, u32[]{:S(2)}) copy-start(pred[32]{0:T(512)(128)(4,1)S(1)} %get-tuple-element.36) | copy-start | bytes 100
  23.0 13.7 %copy-start.18 = (s32[6912]{0:T(1024)}, s32[6912]{0:T(1024)S(1)}, u32[]{:S(2)}) copy-start(s32[6912]{0:T(1024)S(1)} %reshape.262) | copy-start | bytes 82948
  23.0 26.8 %copy-start.19 = (s32[1024]{0:T(1024)}, s32[1024]{0:T(1024)S(1)}, u32[]{:S(2)}) copy-start(s32[1024]{0:T(1024)S(1)} %pad_clamp_fusion.2) | copy-start | bytes 12292
  28.1 4.4 %collective-permute-start = (bf16[64,32]{0,1:T(8,128)(2,1)S(1)}, bf16[64,32]{0,1:T(8,128)(2,1)S(1)}, u32[]{:S(2)}, u32[]{:S(2)}) collective-permute-start(bf16[64,32]{0,1:T(8,128)(2,1)S(1)} %select_bitcast_fusion.4), channel_id=1, source_target_pairs={{0,4},{4,8},{8,12},{12,16},{16,20},{20,24},{24,28},{1,5},{5,9},{9,... | collective-permute-start | bytes 12296 | tf_op jit(solution)/shard_map/ppermute | solution.py:14
  31.2 5.5 %collective-permute-start.1 = (bf16[64,32]{0,1:T(8,128)(2,1)S(1)}, bf16[64,32]{0,1:T(8,128)(2,1)S(1)}, u32[]{:S(2)}, u32[]{:S(2)}) collective-permute-start(bf16[64,32]{0,1:T(8,128)(2,1)S(1)} %select_bitcast_fusion.3), channel_id=1, source_target_pairs={{4,0},{8,4},{12,8},{16,12},{20,16},{24,20},{28,24},{5,1},{9,5},{13... | collective-permute-start | bytes 12296 | tf_op jit(solution)/shard_map/ppermute | solution.py:17
  32.5 17.3 %copy-start.6 = (s32[7168]{0:T(1024)}, s32[7168]{0:T(1024)S(1)}, u32[]{:S(2)}) copy-start(s32[7168]{0:T(1024)S(1)} %pad_clamp_fusion) | copy-start | bytes 86020
  50.7 22.2 %copy-start.10 = (s32[64,256]{1,0:T(8,128)S(1)}, s32[64,256]{1,0:T(8,128)}, u32[]{:S(2)}) copy-start(s32[64,256]{1,0:T(8,128)} %param.17) | copy-start | bytes 196612
  50.7 24.6 %copy-start.23 = (pred[32]{0:T(512)(128)(4,1)S(1)}, pred[32]{0:T(512)(128)(4,1)}, u32[]{:S(2)}) copy-start(pred[32]{0:T(512)(128)(4,1)} %copy-done.22) | copy-start | bytes 100
  50.7 28.2 %copy-start.21 = (pred[32]{0:T(512)(128)(4,1)S(1)}, pred[32]{0:T(512)(128)(4,1)}, u32[]{:S(2)}) copy-start(pred[32]{0:T(512)(128)(4,1)} %copy-done.20) | copy-start | bytes 100
  50.7 34.0 %copy-start.7 = (s32[7168]{0:T(1024)S(1)}, s32[7168]{0:T(1024)}, u32[]{:S(2)}) copy-start(s32[7168]{0:T(1024)} %copy-done.6) | copy-start | bytes 86020
  53.6 66.6 %reduce-scatter.9.cloned.1.call-start = ((), (), s32[]{:S(2)}) async-start(), calls=%async_computation.6 | async-start | bytes 327680 | tf_op jit(solution)/shard_map/reduce_scatter | solution.py:39
  75.4 4.8 %collective-permute-start.2 = (bf16[64,32]{1,0:T(8,128)(2,1)S(1)}, bf16[64,32]{1,0:T(8,128)(2,1)S(1)}, u32[]{:S(2)}, u32[]{:S(2)}) collective-permute-start(bf16[64,32]{1,0:T(8,128)(2,1)S(1)} %select_bitcast_fusion.2), channel_id=1, source_target_pairs={{0,4},{4,8},{8,12},{12,16},{16,20},{20,24},{24,28},{1,5},{5,9},{9,... | collective-permute-start | bytes 12296 | tf_op jit(solution)/shard_map/ppermute | solution.py:14
  78.9 5.6 %collective-permute-start.3 = (bf16[64,32]{1,0:T(8,128)(2,1)S(1)}, bf16[64,32]{1,0:T(8,128)(2,1)S(1)}, u32[]{:S(2)}, u32[]{:S(2)}) collective-permute-start(bf16[64,32]{1,0:T(8,128)(2,1)S(1)} %select_bitcast_fusion.1), channel_id=1, source_target_pairs={{4,0},{8,4},{12,8},{16,12},{20,16},{24,20},{28,24},{5,1},{9,5},{13... | collective-permute-start | bytes 12296 | tf_op jit(solution)/shard_map/ppermute | solution.py:17
  98.7 21.5 %copy-start.13 = (s32[64,256]{1,0:T(8,128)S(1)}, s32[64,256]{1,0:T(8,128)}, u32[]{:S(2)}) copy-start(s32[64,256]{1,0:T(8,128)} %param.18) | copy-start | bytes 196612
  98.7 21.5 %copy-start.16 = (bf16[64,256]{1,0:T(8,128)(2,1)S(1)}, bf16[64,256]{1,0:T(8,128)(2,1)}, u32[]{:S(2)}) copy-start(bf16[64,256]{1,0:T(8,128)(2,1)} %param.21) | copy-start | bytes 98308
  100.1 225.8 %all-reduce.3.cloned.1.call-start = ((), (), s32[]{:S(2)}) async-start(), calls=%async_computation.7 | async-start | bytes 7077888 | tf_op jit(solution)/shard_map/psum | solution.py:130
  100.7 20.4 %copy-start.8 = (bf16[64,256]{1,0:T(8,128)(2,1)}, bf16[64,256]{1,0:T(8,128)(2,1)S(1)}, u32[]{:S(2)}) copy-start(bf16[64,256]{1,0:T(8,128)(2,1)S(1)} %copy.99) | copy-start | bytes 98308
  169.2 7.4 %collective-permute-start.4 = (f32[64,32]{0,1:T(8,128)S(1)}, f32[64,32]{0,1:T(8,128)S(1)}, u32[]{:S(2)}, u32[]{:S(2)}) collective-permute-start(f32[64,32]{0,1:T(8,128)S(1)} %get-tuple-element.45), channel_id=1, source_target_pairs={{0,4},{4,8},{8,12},{12,16},{16,20},{20,24},{24,28},{1,5},{5,9},{9,... | collective-permute-start | bytes 24584 | tf_op jit(solution)/shard_map/ppermute | solution.py:14
  172.6 5.8 %collective-permute-start.5 = (f32[64,32]{0,1:T(8,128)S(1)}, f32[64,32]{0,1:T(8,128)S(1)}, u32[]{:S(2)}, u32[]{:S(2)}) collective-permute-start(f32[64,32]{0,1:T(8,128)S(1)} %get-tuple-element.44), channel_id=1, source_target_pairs={{4,0},{8,4},{12,8},{16,12},{20,16},{24,20},{28,24},{5,1},{9,5},{13... | collective-permute-start | bytes 24584 | tf_op jit(solution)/shard_map/ppermute | solution.py:17
  188.2 47.3 %copy-start.9 = (bf16[64,256]{1,0:T(8,128)(2,1)S(1)}, bf16[64,256]{1,0:T(8,128)(2,1)}, u32[]{:S(2)}) copy-start(bf16[64,256]{1,0:T(8,128)(2,1)} %copy-done.8) | copy-start | bytes 98308
  188.2 47.3 %copy-start.14 = (s32[64,256]{1,0:T(8,128)S(1)}, s32[64,256]{1,0:T(8,128)}, u32[]{:S(2)}) copy-start(s32[64,256]{1,0:T(8,128)} %param.18) | copy-start | bytes 196612
  188.2 47.3 %copy-start.15 = (f32[64,256]{1,0:T(8,128)S(1)}, f32[64,256]{1,0:T(8,128)}, u32[]{:S(2)}) copy-start(f32[64,256]{1,0:T(8,128)} %reduce-scatter.9.cloned.1.call-done) | copy-start | bytes 196612
  188.2 47.3 %copy-start.17 = (bf16[64,256]{1,0:T(8,128)(2,1)S(1)}, bf16[64,256]{1,0:T(8,128)(2,1)}, u32[]{:S(2)}) copy-start(bf16[64,256]{1,0:T(8,128)(2,1)} %param.21) | copy-start | bytes 98308
  190.7 56.7 %copy-start.27 = (s32[128,1]{0,1:T(1,128)S(1)}, s32[128,1]{0,1:T(1,128)}, u32[]{:S(2)}) copy-start(s32[128,1]{0,1:T(1,128)} %copy-done.26) | copy-start | bytes 1540
  190.7 64.7 %copy-start.25 = (pred[128]{0:T(512)(128)(4,1)S(1)}, pred[128]{0:T(512)(128)(4,1)}, u32[]{:S(2)}) copy-start(pred[128]{0:T(512)(128)(4,1)} %get-tuple-element.34) | copy-start | bytes 388
  229.9 6.4 %collective-permute-start.6 = (f32[64,32]{0,1:T(8,128)S(1)}, f32[64,32]{0,1:T(8,128)S(1)}, u32[]{:S(2)}, u32[]{:S(2)}) collective-permute-start(f32[64,32]{0,1:T(8,128)S(1)} %get-tuple-element.43), channel_id=1, source_target_pairs={{0,4},{4,8},{8,12},{12,16},{16,20},{20,24},{24,28},{1,5},{5,9},{9,... | collective-permute-start | bytes 24584 | tf_op jit(solution)/shard_map/ppermute | solution.py:14
  234.2 5.6 %collective-permute-start.7 = (f32[64,32]{0,1:T(8,128)S(1)}, f32[64,32]{0,1:T(8,128)S(1)}, u32[]{:S(2)}, u32[]{:S(2)}) collective-permute-start(f32[64,32]{0,1:T(8,128)S(1)} %get-tuple-element.42), channel_id=1, source_target_pairs={{4,0},{8,4},{12,8},{16,12},{20,16},{24,20},{28,24},{5,1},{9,5},{13... | collective-permute-start | bytes 24584 | tf_op jit(solution)/shard_map/ppermute | solution.py:17
  241.4 13.2 %all-to-all-start.2 = ((bf16[8,2,1024]{2,1,0:T(2,128)(2,1)}), bf16[8,2,1024]{2,1,0:T(2,128)(2,1)S(1)}, u32[]{:S(2)}, u32[]{:S(2)}) async-start(bf16[8,2,1024]{2,1,0:T(2,128)(2,1)} %reshape.299), calls=%async_computation.2 | async-start | bytes 65536 | tf_op jit(solution)/shard_map/all_to_all | solution.py:136
  (10 other events, 56.2 us)
Sparse Core Ops, SparseCore 0:
  53.7 19.1 reduce-scatter.6
  100.2 19.9 reduce-scatter.8
  186.7 139.0 all-reduce.2
where the time goes:
time: 337 us; the launch traced here: 336 us
  waiting for transfers between devices  121 us (36%)
  other arithmetic  95 us (28%)
  local copies, waits for them, and re-layouts  43.5 us (13%)
  starting transfers between devices  32.2 us (10%)
  blocking collectives  21 us (6%)
  between operations  14.5 us (4%)
  matrix products  8.63 us (3%)
    scatter-add x2, other arithmetic, adjoint(): jnp.zeros((pushed.shape[0], extent), jnp.float32).at[:, kernel_map]  78.2 us
    psum x1, waiting for transfers between devices, local(): lax.psum((weight_grad_first, weight_grad_second), 'brick')  69.7 us
    reduce_scatter x2, waiting for transfers between devices, convolve(): lax.psum_scatter(jnp.einsum('ckr,kco->or', gathered, weight, preferred_el...  28.3 us
    gather x4, local copies, waits for them, and re-layouts, convolve(): gathered = jnp.take(extended, kernel_map, axis=1, mode='fill', fill_value=0)  27.8 us
    ppermute x4, starting transfers between devices, with_halo(): lax.ppermute(lax.slice_in_dim(block, block.shape[dim] - width, None, axis...  13.4 us
    ppermute x4, waiting for transfers between devices, with_halo(): lax.ppermute(lax.slice_in_dim(block, 0, width, axis=dim), axis, backward)  11.9 us
    all_gather x2, blocking collectives, adjoint(): gathered_grad = lax.all_gather(grad_local, 'ch', axis=0, tiled=True)  11 us
    all_to_all x1, blocking collectives, local(): lax.all_to_all(tallies, 'brick', split_axis=1, concat_axis=1, tiled=True)  10 us
  transfers between devices with their start and end apart: 13, of which 9 were waited for; matrix products, arithmetic and copies ran while one was open for 17% of the time, Pallas kernels for 0%

commit v1 on v0

--- a/solution.py
+++ b/solution.py
@@ -1,9 +1,577 @@
+import functools
+
 import jax
 import jax.numpy as jnp
 from jax import lax
+from jax.experimental import pallas as pl
+from jax.experimental.pallas import tpu as pltpu
 from jax.sharding import PartitionSpec as P
 
 KEEP_RATE = 0.9
+BF = jnp.bfloat16
+F32 = jnp.float32
+INTERPRET = False
+
+
+def slope_silu(value):
+    sig = jax.nn.sigmoid(value)
+    return sig * (1.0 + value * (1.0 - sig))
+
+
+def nn(a, b):
+    return lax.dot_general(a, b, (((1,), (0,)), ((), ())), preferred_element_type=F32)
+
+
+def nt(a, b):
+    return lax.dot_general(a, b, (((1,), (1,)), ((), ())), preferred_element_type=F32)
+
+
+def hot(index_row, rows):
+    shape = (rows, index_row.shape[1])
+    row = lax.broadcasted_iota(jnp.int32, shape, 0)
+    return jnp.where(row == index_row, 1.0, 0.0).astype(BF)
+
+
+def loop(count, step, carry, group=3):
+    group = group if count % group == 0 else 1
+
+    def body(i, carry):
+        for j in range(group):
+            carry = step(i * group + j, carry)
+        return carry
+
+    return lax.fori_loop(0, count // group, body, carry)
+
+
+def call(kernel, outs, scratch, args, ids, flops=10**9, vmem=40, name=None):
+    single = not isinstance(outs, (list, tuple))
+    outs = [outs] if single else list(outs)
+    moved = sum(a.size * a.dtype.itemsize for a in args)
+    moved += sum(o.size * jnp.dtype(o.dtype).itemsize for o in outs)
+    result = pl.pallas_call(
+        kernel,
+        out_shape=outs,
+        in_specs=[pl.BlockSpec(memory_space=pltpu.SMEM)]
+        + [pl.BlockSpec(memory_space=pltpu.VMEM)] * len(args),
+        out_specs=[pl.BlockSpec(memory_space=pltpu.VMEM)] * len(outs),
+        scratch_shapes=scratch,
+        compiler_params=None
+        if INTERPRET
+        else pltpu.CompilerParams(vmem_limit_bytes=vmem * 2**20),
+        cost_estimate=pl.CostEstimate(flops=flops, bytes_accessed=moved, transcendentals=0),
+        interpret=INTERPRET,
+        name=name,
+    )(ids, *args)
+    return result[0] if single else result
+
+
+class Sizes:
+    def __init__(self, features, kernel_map, send_lists, nb, nc):
+        self.nb, self.nc = nb, nc
+        self.ch, self.scan = features.shape
+        self.koff, self.slots = kernel_map.shape
+        self.rim = send_lists.shape[1]
+        self.cap = self.slots // nb
+        self.hs = 4 * self.rim
+        self.half = self.ch // 2
+        self.kr = -(-(self.koff + 1) // 16) * 16
+        self.rows = 2 * self.half + self.kr
+        self.ext = self.slots + 2 * self.rim
+        self.shift = self.ext // 2
+        self.all = self.ch * nc
+        self.depth = self.koff * self.ch
+
+
+def pack_kernel(z, ids, feat, table, drop, out):
+    h, lanes = z.half, z.scan
+    out[0:h, 0:lanes] = feat[0:h, :]
+    out[0:h, lanes : 2 * lanes] = feat[h : 2 * h, :]
+    lend = hot(table[z.koff : z.koff + 1, lanes : lanes + z.hs], z.slots)
+    chosen = nn(drop[...].astype(F32).astype(BF), lend).astype(BF)
+    out[h : 2 * h, 0 : z.hs] = chosen[0:h, :]
+    out[h : 2 * h, z.hs : 2 * z.hs] = chosen[h : 2 * h, :]
+    row = lax.broadcasted_iota(jnp.int32, (z.kr, z.slots), 0)
+    value = table[...] - jnp.where(row < z.koff, z.shift, 0)
+    out[2 * h :, :] = value.astype(F32).astype(BF)
+
+
+def read_table(z, pay, brick):
+    return pay[brick, 2 * z.half :, :].astype(F32)
+
+
+def lanes_of(shape):
+    return lax.broadcasted_iota(jnp.int32, shape, len(shape) - 1)
+
+
+def meta_row(z, pay, brick):
+    return read_table(z, pay, brick)[z.koff : z.koff + 1, :].astype(jnp.int32)
+
+
+def map_values(z, pay, brick):
+    return read_table(z, pay, brick).astype(jnp.int32) + z.shift
+
+
+def own_index(z, value):
+    return value - z.rim
+
+
+def halo_index(z, value):
+    high = jnp.where(value >= z.rim + z.slots, value - z.slots + z.rim, -1)
+    return jnp.where(value < z.rim, value + z.rim, high)
+
+
+def gather_own(z, dst, table, halo, kmo, kmh):
+    def step(k, carry):
+        oh = hot(kmo[pl.ds(k, 1), :], z.slots)
+        hh = hot(kmh[pl.ds(k, 1), :], z.hs)
+        got = nn(table, oh) + nn(halo, hh)
+        dst[pl.ds(pl.multiple_of(k * z.ch, z.ch), z.ch), 0 : z.slots] = got.astype(BF)
+        return carry
+
+    loop(z.koff, step, 0)
+
+
+def halo_of(z, lent, a):
+    lane = lanes_of(lent.shape[1:])
+    none = jnp.zeros(lent.shape[1:], F32)
+    low = lent[a - 1].astype(F32) if a > 0 else none
+    high = lent[a + 1].astype(F32) if a < z.nb - 1 else none
+    return jnp.where(lane < 2 * z.rim, low, high).astype(BF)
+
+
+def first_kernel(z, ids, near, far, drop, wt, *rest):
+    outs, (own, lent, stack, kmo, kmh, klo, klh) = rest[:-7], rest[-7:]
+    parts, (keep, pay, vox, halo) = outs[: z.nc], outs[z.nc :]
+    b, c = ids[0], ids[1]
+    for q in range(z.nb):
+        pay[b ^ q] = (near if q % 2 == 0 else far)[q // 2]
+    for s in range(z.nb):
+        own[s : s + 1, :] = read_table(z, pay, s)[z.koff : z.koff + 1, 0 : z.scan]
+    columns = jnp.transpose(own[...])
+    lane = lanes_of((z.scan, z.scan))
+    sub = lax.broadcasted_iota(jnp.int32, (z.scan, z.scan), 0)
+    key_lane = lanes_of((z.scan, z.slots)).astype(F32)
+    ones = jnp.ones((16, z.scan), BF)
+    for s in range(z.nb):
+        mine = columns[:, s : s + 1]
+        earlier = (mine == own[s : s + 1, :]) & (lane < sub)
+        ordinal = jnp.sum(jnp.where(earlier, 1.0, 0.0), axis=1, keepdims=True)
+        key = mine * z.cap + ordinal
+        placed = jnp.where(key == key_lane, 1.0, 0.0).astype(BF)
+        h = z.half
+        rows = jnp.concatenate(
+            [pay[s, 0:h, 0 : z.scan], pay[s, 0:h, z.scan : 2 * z.scan], ones], axis=0
+        )
+        moved = nn(rows, placed).astype(BF)
+        for a in range(z.nb):
+            vox[a, :, s * z.cap : (s + 1) * z.cap] = moved[:, a * z.cap : (a + 1) * z.cap]
+    for a in range(z.nb):
+        lend = hot(meta_row(z, pay, a)[:, z.scan : z.scan + z.hs], z.slots)
+        lent[a] = nn(vox[a], lend).astype(BF)
+    for a in range(z.nb):
+        halo[a] = halo_of(z, lent, a)
+    before, after = jnp.maximum(b - 1, 0), jnp.minimum(b + 1, z.nb - 1)
+    value = map_values(z, pay, b)
+    kmo[...] = own_index(z, value)
+    kmh[...] = halo_index(z, value)
+    hl = lanes_of((z.kr, z.hs))
+    from_before = nn(
+        pay[before, 2 * z.half :, :],
+        hot(meta_row(z, pay, before)[:, z.scan : z.scan + z.hs], z.slots),
+    )
+    from_after = nn(
+        pay[after, 2 * z.half :, :],
+        hot(meta_row(z, pay, after)[:, z.scan : z.scan + z.hs], z.slots),
+    )
+    later = hl >= 2 * z.rim
+    value = jnp.where(later, from_after, from_before).astype(jnp.int32) + z.shift
+    index = own_index(z, value)
+    inside = (index >= 0) & (index < z.slots)
+    klo[...] = jnp.where(inside, index + jnp.where(later, z.slots, 0), -1)
+    index = halo_index(z, value)
+    klh[...] = jnp.where(index >= 0, index + jnp.where(later, z.hs, 0), -1)
+    gather_own(z, stack, vox[b, 0 : z.ch, :], halo[b, 0 : z.ch, :], kmo, kmh)
+    pair = jnp.concatenate([vox[before, 0 : z.ch, :], vox[after, 0 : z.ch, :]], axis=1)
+    pair_halo = jnp.concatenate([halo[before, 0 : z.ch, :], halo[after, 0 : z.ch, :]], axis=1)
+
+    def step(k, carry):
+        oh = hot(klo[pl.ds(k, 1), :], 2 * z.slots)
+        hh = hot(klh[pl.ds(k, 1), :], 2 * z.hs)
+        got = nn(pair, oh) + nn(pair_halo, hh)
+        rows = pl.ds(pl.multiple_of(k * z.ch, z.ch), z.ch)
+        stack[rows, z.slots : z.slots + z.hs] = got.astype(BF)
+        return carry
+
+    loop(z.koff, step, 0)
+    h = z.half
+    kept = drop[...].astype(F32) * vox[b, z.ch : z.ch + 1, :].astype(F32)
+    keep[:, 0 : z.slots] = kept / KEEP_RATE
+    pick_before = jnp.concatenate([pay[before, h : 2 * h, 0 : z.hs], pay[before, h : 2 * h, z.hs : 2 * z.hs]], axis=0)
+    pick_after = jnp.concatenate([pay[after, h : 2 * h, 0 : z.hs], pay[after, h : 2 * h, z.hs : 2 * z.hs]], axis=0)
+    lane = lanes_of((z.ch, z.hs))
+    picked = jnp.where(lane < 2 * z.rim, pick_before.astype(F32), pick_after.astype(F32))
+    keep[:, z.slots :] = picked * halo[b, z.ch : z.ch + 1, :].astype(F32) / KEEP_RATE
+    for j in range(z.nc):
+        rows = pl.ds(pl.multiple_of((c ^ j) * z.ch, z.ch), z.ch)
+        parts[j][...] = nn(wt[rows, :], stack[...]).astype(parts[j].dtype)
+
+
+def second_kernel(z, ids, *rest):
+    arrived, (keep, kmap, wt) = rest[: z.nc], rest[z.nc : z.nc + 3]
+    outs, (stack, kmo, kmh) = rest[z.nc + 3 : -3], rest[-3:]
+    parts, (conv, hidden) = outs[: z.nc], outs[z.nc :]
+    c = ids[1]
+    total = arrived[0][...]
+    for part in arrived[1:]:
+        total = total + part[...].astype(F32)
+    made = (total * jax.nn.sigmoid(total) * keep[...]).astype(BF)
+    conv[...] = total[:, 0 : z.slots]
+    hidden[...] = made[:, 0 : z.slots]
+    kmo[...] = own_index(z, kmap[...])
+    kmh[...] = halo_index(z, kmap[...])
+    gather_own(z, stack, made[:, 0 : z.slots], made[:, z.slots :], kmo, kmh)
+    for j in range(z.nc):
+        rows = pl.ds(pl.multiple_of((c ^ j) * z.ch, z.ch), z.ch)
+        parts[j][...] = nn(wt[rows, :], stack[...]).astype(parts[j].dtype)
+
+
+def third_kernel(z, ids, *rest):
+    arrived, (vox, drop, cot) = rest[: z.nc], rest[z.nc : z.nc + 3]
+    block, sends = rest[z.nc + 3], rest[z.nc + 4 :]
+    b = ids[0]
+    total = arrived[0][...]
+    for part in arrived[1:]:
+        total = total + part[...].astype(F32)
+    keep = drop[...].astype(F32) * vox[b, z.ch : z.ch + 1, :].astype(F32) / KEEP_RATE
+    summed = vox[b, 0 : z.ch, :].astype(F32) + keep * total
+    block[...] = (summed * jax.nn.sigmoid(summed)).astype(BF)
+    pre = cot[...].astype(F32) * slope_silu(summed)
+    grad = (pre * keep).astype(BF)
+    pre = pre.astype(BF)
+    lane = lanes_of((1, 2 * z.cap))
+    for i, send in enumerate(sends):
+        first, other = b ^ (2 * i), b ^ (2 * i + 1)
+        index = jnp.where(lane < z.cap, first * z.cap + lane, (other - 1) * z.cap + lane)
+        send[:, 0 : z.slots] = grad
+        send[:, z.slots :] = nn(pre, hot(index, z.slots)).astype(BF)
+
+
+def collect(z, dst, ids, near, far):
+    b, c = ids[0], ids[1]
+    nz = z.nb // 2
+    for i in range(z.nc // 2):
+        for y in range(2):
+            for k in range(nz):
+                at = (i * 2 + y) * nz + k
+                for low, source in ((0, near), (1, far)):
+                    rows = pl.ds(pl.multiple_of((c ^ (2 * i + low)) * z.ch, z.ch), z.ch)
+                    dst[b ^ (2 * k + y), rows, :] = source[at, :, 0 : z.slots]
+
+
+def push(z, dst, weight, grad):
+    count = z.koff
+    size = z.depth // count
+
+    def step(i, carry):
+        rows = pl.ds(pl.multiple_of(i * size, size), size)
+        dst[rows, :] = nn(weight[rows, :], grad).astype(BF)
+        return carry
+
+    loop(count, step, 0)
+
+
+def fourth_kernel(z, ids, near, far, weight, pay, conv, keep, grad, gall, scan, pushed, kmo, kma, kmb):
+    b = ids[0]
+    collect(z, gall, ids, near, far)
+    nz = z.nb // 2
+    for q in range(z.nb):
+        start = z.slots + (q % 2) * z.cap
+        scan[b ^ q] = near[(q % 2) * nz + q // 2, :, start : start + z.cap]
+    before, after = jnp.maximum(b - 1, 0), jnp.minimum(b + 1, z.nb - 1)
+    push(z, pushed.at[0], weight, gall[b])
+    push(z, pushed.at[1], weight, gall[before])
+    push(z, pushed.at[2], weight, gall[after])
+    kmo[...] = own_index(z, map_values(z, pay, b))
+    value = map_values(z, pay, before)
+    inside = (value >= z.rim + z.slots) & (value < z.ext) & (b > 0)
+    kmb[...] = jnp.where(inside, value - z.slots + z.rim, -1)
+    value = map_values(z, pay, after)
+    kma[...] = jnp.where((value < z.rim) & (b < z.nb - 1), value + z.rim, -1)
+
+    def step(k, carry):
+        total, border = carry
+        rows = pl.ds(pl.multiple_of(k * z.ch, z.ch), z.ch)
+        one = pl.ds(k, 1)
+        total = total + nt(pushed[0, rows, :], hot(kmo[one, :], z.slots))
+        border = border + nt(pushed[1, rows, :], hot(kmb[one, :], z.hs))
+        border = border + nt(pushed[2, rows, :], hot(kma[one, :], z.hs))
+        return total, border
+
+    total, border = loop(
+        z.koff, step, (jnp.zeros((z.ch, z.slots), F32), jnp.zeros((z.ch, z.hs), F32))
+    )
+    lend = hot(meta_row(z, pay, b)[:, z.scan : z.scan + z.hs], z.slots)
+    high = border.astype(BF)
+    total = total + nt(high, lend) + nt((border - high.astype(F32)).astype(BF), lend)
+    grad[...] = (total * keep[:, 0 : z.slots] * slope_silu(conv[...])).astype(BF)
+
+
+def weight_sum(z, out, total, stack, kmo, kmh, table_at, halo_at, pay, gall):
+    factor = float(z.nb * z.slots) ** (-0.5)
+    pieces = 9 if z.koff % 9 == 0 else z.koff
+    size = z.depth // pieces
+
+    def brick(a, carry):
+        value = map_values(z, pay, a)
+        kmo[...] = own_index(z, value)
+        kmh[...] = halo_index(z, value)
+        gather_own(z, stack, table_at(a), halo_at(a), kmo, kmh)
+        grads = gall[a]
+
+        def piece(i, carry):
+            rows = pl.ds(pl.multiple_of(i * size, size), size)
+            total[rows, :] = total[rows, :] + nt(stack[rows, :], grads)
+            return carry
+
+        return loop(pieces, piece, carry)
+
+    total[...] = jnp.zeros_like(total)
+    lax.fori_loop(0, z.nb, brick, 0)
+    out[...] = (total[...] * factor).astype(BF)
+
+
+def second_weight_kernel(z, ids, near, far, pay, gall, out, total, stack, kmo, kmh, table, lent, halo):
+    b = ids[0]
+    for q in range(z.nb):
+        table[b ^ q] = (near if q % 2 == 0 else far)[q // 2]
+    for a in range(z.nb):
+        lend = hot(meta_row(z, pay, a)[:, z.scan : z.scan + z.hs], z.slots)
+        lent[a] = nn(table[a], lend).astype(BF)
+    for a in range(z.nb):
+        halo[a] = halo_of(z, lent, a)
+    weight_sum(z, out, total, stack, kmo, kmh, lambda a: table[a], lambda a: halo[a], pay, gall)
+
+
+def last_kernel(z, ids, near, far, weight, pay, vox, halo, scan, owner, out, wout, gall, pushed, total, stack, kmo, kmh):
+    b = ids[0]
+    collect(z, gall, ids, near, far)
+    mine = owner[...].astype(F32)
+    row = read_table(z, pay, b)[z.koff : z.koff + 1, 0 : z.scan]
+    square = (z.scan, z.scan)
+    lane = lanes_of(square)
+    sub = lax.broadcasted_iota(jnp.int32, square, 0)
+    earlier = (mine == row) & (lane < sub)
+    ordinal = jnp.sum(jnp.where(earlier, 1.0, 0.0), axis=1, keepdims=True)
+    slot = ordinal + (b * z.cap).astype(F32)
+    at = lax.broadcasted_iota(jnp.int32, (z.hs, z.slots), 0)
+    wanted = jnp.where(at < z.rim, z.rim + b * z.cap + at, -5)
+    if z.cap < z.rim:
+        wanted = jnp.where(at < z.cap, wanted, -5)
+    wanted = jnp.where((at >= z.rim) & (at < 2 * z.rim), at - z.rim, wanted)
+    wanted = jnp.where((at >= 2 * z.rim) & (at < 3 * z.rim), at + z.slots - z.rim, wanted)
+    target = lanes_of((1, z.hs))
+
+    def brick(a, result):
+        push(z, pushed, weight, gall[a])
+        kmo[...] = map_values(z, pay, a)
+
+        def step(k, got):
+            rows = pl.ds(pl.multiple_of(k * z.ch, z.ch), z.ch)
+            chosen = jnp.where(wanted == kmo[pl.ds(k, 1), :], 1.0, 0.0).astype(BF)
+            return got + nt(pushed[rows, :], chosen)
+
+        got = loop(z.koff, step, jnp.zeros((z.ch, z.hs), F32))
+        before, after = jnp.maximum(a - 1, 0), jnp.minimum(a + 1, z.nb - 1)
+        low = meta_row(z, pay, before)[:, z.scan : z.scan + z.hs]
+        high = meta_row(z, pay, after)[:, z.scan : z.scan + z.hs]
+        holder = jnp.where(target < z.rim, a, jnp.where(target < 2 * z.rim, a - 1, a + 1))
+        where = jnp.where(target < z.rim, b * z.cap + target, jnp.where(target < 2 * z.rim, low, high))
+        place = jnp.where((mine == holder.astype(F32)) & (slot == where.astype(F32)), 1.0, 0.0).astype(BF)
+        big = got.astype(BF)
+        result = result + nt(big, place) + nt((got - big.astype(F32)).astype(BF), place)
+        target_own = lanes_of((1, z.cap))
+        place = jnp.where((mine == jnp.asarray(a, F32)) & (ordinal == target_own.astype(F32)), 1.0, 0.0).astype(BF)
+        return result + nt(scan[a], place)
+
+    result = lax.fori_loop(0, z.nb, brick, jnp.zeros((z.ch, z.scan), F32))
+    out[...] = result.astype(BF)
+    weight_sum(z, wout, total, stack, kmo, kmh, lambda a: vox[a, 0 : z.ch, :], lambda a: halo[a, 0 : z.ch, :], pay, gall)
+
+
+def swap(value, axis, mask):
+    count = lax.axis_size(axis)
+    return lax.ppermute(value, axis, [(i ^ mask, i) for i in range(count)])
+
+
+def swap_both(value, brick_mask, ch_mask):
+    if ch_mask == 0:
+        return swap(value, "brick", brick_mask)
+    if brick_mask == 0:
+        return swap(value, "ch", ch_mask)
+    nb, nc = lax.axis_size("brick"), lax.axis_size("ch")
+    pairs = [
+        ((b ^ brick_mask) * nc + (c ^ ch_mask), b * nc + c) for b in range(nb) for c in range(nc)
+    ]
+    return lax.ppermute(value, ("brick", "ch"), pairs)
+
+
+def over_even(blocks, count):
+    return jnp.stack(
+        [blocks[0]] + [swap(blocks[i], "brick", 2 * i) for i in range(1, count // 2)]
+    )
+
+
+def over_bricks(block, nb):
+    near = over_even([block] * (nb // 2), nb)
+    return near, swap(near, "brick", 1)
+
+
+def over_all(blocks, nb, nc):
+    plane = over_even(blocks, nb)
+    parts = [plane]
+    for i in range(nc // 2):
+        for y in range(2):
+            if i or y:
+                parts.append(swap_both(plane, y, 2 * i))
+    near = jnp.concatenate(parts, axis=0)
+    return near, swap(near, "ch", 1)
+
+
+def gathered_local(
+    features,
+    owner_map,
+    kernel_map,
+    send_lists,
+    drop_first,
+    drop_second,
+    weight_first,
+    weight_second,
+    cotangent,
+):
+    nb, nc = lax.axis_size("brick"), lax.axis_size("ch")
+    z = Sizes(features, kernel_map, send_lists, nb, nc)
+    ids = jnp.stack([lax.axis_index("brick"), lax.axis_index("ch")]).astype(jnp.int32)
+    sds = jax.ShapeDtypeStruct
+    vm = pltpu.VMEM
+    pad = jnp.full((1, z.rim), -1, jnp.int32)
+    meta = jnp.concatenate([owner_map.reshape(1, z.scan), pad, send_lists[1:2], send_lists[0:1], pad], axis=1)
+    table = jnp.concatenate(
+        [kernel_map, meta, jnp.zeros((z.kr - z.koff - 1, z.slots), jnp.int32)], axis=0
+    )
+    flat_first = weight_first.reshape(z.depth, z.all)
+    flat_second = weight_second.reshape(z.depth, z.all)
+    turned_first = flat_first.T
+    turned_second = flat_second.T
+
+    payload = call(
+        functools.partial(pack_kernel, z),
+        sds((z.rows, z.slots), BF),
+        [],
+        [features, table, drop_first],
+        ids,
+        name="pack",
+    )
+    near, far = over_bricks(payload, nb)
+    wide = z.slots + z.hs
+    ints = [vm((z.kr, z.slots), jnp.int32)] * 2
+    *parts, keep, pay, vox, halo = call(
+        functools.partial(first_kernel, z),
+        [sds((z.ch, wide), F32)]
+        + [sds((z.ch, wide), BF)] * (nc - 1)
+        + [
+            sds((z.ch, wide), F32),
+            sds((nb, z.rows, z.slots), BF),
+            sds((nb, z.ch + 16, z.slots), BF),
+            sds((nb, z.ch + 16, z.hs), BF),
+        ],
+        [
+            vm((nb, z.scan), F32),
+            vm((nb, z.ch + 16, z.hs), BF),
+            vm((z.depth, wide), BF),
+            *ints,
+            vm((z.kr, z.hs), jnp.int32),
+            vm((z.kr, z.hs), jnp.int32),
+        ],
+        [near, far, drop_first, turned_first],
+        ids,
+        name="first",
+    )
+    arrived = [parts[0]] + [swap(parts[j], "ch", j) for j in range(1, nc)]
+    small = [vm((z.koff, z.slots), jnp.int32)] * 2
+    *parts, conv, hidden = call(
+        functools.partial(second_kernel, z),
+        [sds((z.ch, z.slots), F32)]
+        + [sds((z.ch, z.slots), BF)] * (nc - 1)
+        + [sds((z.ch, z.slots), F32), sds((z.ch, z.slots), BF)],
+        [vm((z.depth, z.slots), BF), *small],
+        [*arrived, keep, kernel_map, turned_second],
+        ids,
+        name="second",
+    )
+    arrived = [parts[0]] + [swap(parts[j], "ch", j) for j in range(1, nc)]
+    block_out, *sends = call(
+        functools.partial(third_kernel, z),
+        [sds((z.ch, z.slots), BF)] + [sds((z.ch, z.slots + 2 * z.cap), BF)] * (nb // 2),
+        [],
+        [*arrived, vox, drop_second, cotangent],
+        ids,
+        name="third",
+    )
+    hidden_near, hidden_far = over_bricks(hidden, nb)
+    near, far = over_all(sends, nb, nc)
+    grad_first, gall, scan = call(
+        functools.partial(fourth_kernel, z),
+        [
+            sds((z.ch, z.slots), BF),
+            sds((nb, z.all, z.slots), BF),
+            sds((nb, z.ch, z.cap), BF),
+        ],
+        [
+            vm((3, z.depth, z.slots), BF),
+            vm((z.kr, z.slots), jnp.int32),
+            vm((z.kr, z.slots), jnp.int32),
+            vm((z.kr, z.slots), jnp.int32),
+        ],
+        [near, far, flat_second, pay, conv, keep],
+        ids,
+        name="fourth",
+    )
+    weight_grad_second = call(
+        functools.partial(second_weight_kernel, z),
+        sds((z.depth, z.all), BF),
+        [
+            vm((z.depth, z.all), F32),
+            vm((z.depth, z.slots), BF),
+            *ints,
+            vm((nb, z.ch, z.slots), BF),
+            vm((nb, z.ch, z.hs), BF),
+            vm((nb, z.ch, z.hs), BF),
+        ],
+        [hidden_near, hidden_far, pay, gall],
+        ids,
+        name="second_weight",
+    )
+    near, far = over_all([grad_first] * (nb // 2), nb, nc)
+    grad_features, weight_grad_first = call(
+        functools.partial(last_kernel, z),
+        [sds((z.ch, z.scan), BF), sds((z.depth, z.all), BF)],
+        [
+            vm((nb, z.all, z.slots), BF),
+            vm((z.depth, z.slots), BF),
+            vm((z.depth, z.all), F32),
+            vm((z.depth, z.slots), BF),
+            *ints,
+        ],
+        [near, far, flat_first, pay, vox, halo, scan, owner_map],
+        ids,
+        name="last",
+    )
+    return (
+        block_out,
+        grad_features,
+        weight_grad_first.reshape(weight_first.shape),
+        weight_grad_second.reshape(weight_second.shape),
+    )
 
 
 def with_halo(block, sides, width):
@@ -19,11 +587,6 @@
     return block
 
 
-def slope_silu(value):
-    sig = jax.nn.sigmoid(value)
-    return sig * (1.0 + value * (1.0 - sig))
-
-
 def spread(field, send_lists):
     rim_width = send_lists.shape[1]
     outgoing = jnp.concatenate(
@@ -69,7 +632,7 @@
     return interior.at[:, send_lists[1]].add(padded[:, 3 * rim_width :])
 
 
-def local(
+def summed_local(
     features,
     owner_map,
     kernel_map,
@@ -150,6 +713,17 @@
     )
 
 
+def local(features, owner_map, kernel_map, *rest):
+    nb, nc = lax.axis_size("brick"), lax.axis_size("ch")
+    channels = features.shape[0]
+    gather = nb * kernel_map.shape[1] <= 2 * kernel_map.shape[0] * channels
+    even = all(n > 1 and n & (n - 1) == 0 for n in (nb, nc))
+    scan, slots, rim = features.shape[1], kernel_map.shape[1], rest[0].shape[1]
+    fits = slots <= nb * rim and slots == 2 * scan and 4 * rim <= scan
+    plan = gathered_local if gather and even and fits else summed_local
+    return plan(features, owner_map, kernel_map, *rest)
+
+
 def solution(mesh):
     return jax.shard_map(
         local,

time: 337 us -> 194 us (0.58)
  Pallas kernels: 0 us -> 107 us
  other arithmetic: 95 us -> 0.26 us
  waiting for transfers between devices: 121 us -> 43.6 us
  local copies, waits for them, and re-layouts: 43.5 us -> 9.6 us
  blocking collectives: 21 us -> 0 us
  between operations: 14.5 us -> 0.86 us
  matrix products: 8.63 us -> 0 us
    pallas_call x0 -> x7, Pallas kernels: none -> 107 us  [call(): pl.pallas_call(kernel, out_shape=outs, in_specs=[pl.BlockSpec(memory_spac...]
    scatter-add x6 -> x0, other arithmetic: 81.6 us -> none  [the longest x2 78.2 us: adjoint(): jnp.zeros((pushed.shape[0], extent), jnp.float32).at[:, kernel_map]]
    psum x1 -> x0, waiting for transfers between devices: 69.7 us -> none  [local(): lax.psum((weight_grad_first, weight_grad_second), 'brick')]
    ppermute x8 -> x28, waiting for transfers between devices: 11.9 us -> 43.6 us  [the longest x26 39.8 us: swap(): return lax.ppermute(value, axis, [(i ^ mask, i) for i in range(count)])]
    gather x11 -> x0, local copies, waits for them, and re-layouts: 31.2 us -> none  [the longest x4 27.8 us: convolve(): gathered = jnp.take(extended, kernel_map, axis=1, mode='fill', fill_value=0)]
    reduce_scatter x2 -> x0, waiting for transfers between devices: 28.3 us -> none  [convolve(): lax.psum_scatter(jnp.einsum('ckr,kco->or', gathered, weight, preferred_el...]
    ppermute x8 -> x28, starting transfers between devices: 18.7 us -> 32.7 us  [the longest x26 30.6 us: swap(): return lax.ppermute(value, axis, [(i ^ mask, i) for i in range(count)])]
    all_to_all x2 -> x0, starting transfers between devices: 13.3 us -> none  [the longest x1 7.31 us: local(): lax.all_to_all(outgoing.reshape(channels, bricks, capacity), 'brick', spl...]
  transfers between devices with their start and end apart: 13 -> 28, of which waited for: 9 -> 21; matrix products, arithmetic and copies ran while one was open for 17% -> 1% of each run, Pallas kernels for 0% -> 13%
where the time goes in v1:
time: 194 us
  Pallas kernels  107 us (55%)
  waiting for transfers between devices  43.6 us (22%)
  starting transfers between devices  32.7 us (17%)
  local copies, waits for them, and re-layouts  9.6 us (5%)
    pallas_call x7, Pallas kernels, call(): pl.pallas_call(kernel, out_shape=outs, in_specs=[pl.BlockSpec(memory_spac...  107 us
    ppermute x26, waiting for transfers between devices, swap(): return lax.ppermute(value, axis, [(i ^ mask, i) for i in range(count)])  39.8 us
    ppermute x26, starting transfers between devices, swap(): return lax.ppermute(value, axis, [(i ^ mask, i) for i in range(count)])  30.6 us
    unnamed x51, local copies, waits for them, and re-layouts  6.77 us
  transfers between devices with their start and end apart: 28, of which 21 were waited for; matrix products, arithmetic and copies ran while one was open for 1% of the time, Pallas kernels for 13%

profile of v1, /device:TPU:0, one launch (start us, length us, event | category | flops | bytes accessed | tf_op | source)
XLA Modules:
  0.0 194.0 jit_solution(13947148107079404031)
XLA Ops:
  3.8 3.1 %collective-permute-start = (bf16[96,256]{1,0:T(8,128)(2,1)S(1)}, bf16[96,256]{1,0:T(8,128)(2,1)S(1)}, u32[]{:S(2)}, u32[]{:S(2)}) collective-permute-start(bf16[96,256]{1,0:T(8,128)(2,1)S(1)} %pack.1), channel_id=1, source_target_pairs={{8,0},{12,4},{0,8},{4,12},{24,16},{28,20},{16,24},{20,28},{9,1},{1... | collective-permute-start | bytes 147464 | tf_op jit(solution)/shard_map/ppermute | solution.py:403
  6.9 2.6 %collective-permute-start.1 = (bf16[96,256]{1,0:T(8,128)(2,1)S(1)}, bf16[96,256]{1,0:T(8,128)(2,1)S(1)}, u32[]{:S(2)}, u32[]{:S(2)}) collective-permute-start(bf16[96,256]{1,0:T(8,128)(2,1)S(1)} %pack.1), channel_id=1, source_target_pairs={{16,0},{20,4},{24,8},{28,12},{0,16},{4,20},{8,24},{12,28},{17,1},{... | collective-permute-start | bytes 147464 | tf_op jit(solution)/shard_map/ppermute | solution.py:403
  9.5 3.3 %collective-permute-done.1 = bf16[96,256]{1,0:T(8,128)(2,1)S(1)} collective-permute-done((bf16[96,256]{1,0:T(8,128)(2,1)S(1)}, bf16[96,256]{1,0:T(8,128)(2,1)S(1)}, u32[]{:S(2)}, u32[]{:S(2)}) %collective-permute-start.1) | collective-permute-done | bytes 49184 | tf_op jit(solution)/shard_map/ppermute | solution.py:403
  12.8 2.6 %collective-permute-done.2 = bf16[96,256]{1,0:T(8,128)(2,1)S(1)} collective-permute-done((bf16[96,256]{1,0:T(8,128)(2,1)S(1)}, bf16[96,256]{1,0:T(8,128)(2,1)S(1)}, u32[]{:S(2)}, u32[]{:S(2)}) %collective-permute-start.2) | collective-permute-done | bytes 49184 | tf_op jit(solution)/shard_map/ppermute | solution.py:403
  15.4 1.6 collective-permute-start.3
  17.6 3.5 %collective-permute-done.3.far = bf16[4,96,256]{2,1,0:T(8,128)(2,1)S(1)} collective-permute-done((bf16[4,96,256]{2,1,0:T(8,128)(2,1)S(1)}, bf16[4,96,256]{2,1,0:T(8,128)(2,1)S(1)}, u32[]{:S(2)}, u32[]{:S(2)}) %collective-permute-start.3) | collective-permute-done | bytes 196640 | tf_op jit(solution)/shard_map/ppermute | solution.py:403
  21.1 8.5 %first.1 = (f32[64,384]{1,0:T(8,128)S(1)}, bf16[64,384]{1,0:T(8,128)(2,1)S(1)}, bf16[64,384]{1,0:T(8,128)(2,1)S(1)}, bf16[64,384]{1,0:T(8,128)(2,1)S(1)}, f32[64...) custom-call(s32[2]{0:T(128)S(1)} %pad_add_fusion.ids, ...), custom_call_target="tpu_custom_call" | custom-call | flops 1000000000 | bytes 2572288 | tf_op jit(solution)/shard_map/first/pallas_call | solution.py:51
  32.3 1.5 collective-permute-start.5
  34.8 1.7 collective-permute-done.5.rest_2_
  39.3 3.6 %second.1 = (f32[64,256]{1,0:T(8,128)S(1)}, bf16[64,256]{1,0:T(8,128)(2,1)S(1)}, bf16[64,256]{1,0:T(8,128)(2,1)S(1)}, bf16[64,256]{1,0:T(8,128)(2,1)S(1)}, f32[6...) custom-call(s32[2]{0:T(128)S(1)} %pad_add_fusion.ids, f32[64,384]{1,0:T(8,128)S(1)} %copy-done.17, ...), custom_call_target="tpu_custom_call" | custom-call | flops 1000000000 | bytes 1518592 | tf_op jit(solution)/shard_map/second/pallas_call | solution.py:51
  44.8 2.3 %collective-permute-done.8.rest_2_ = bf16[64,256]{1,0:T(8,128)(2,1)S(1)} collective-permute-done((bf16[64,256]{1,0:T(8,128)(2,1)S(1)}, bf16[64,256]{1,0:T(8,128)(2,1)S(1)}, u32[]{:S(2)}, u32[]{:S(2)}) %collective-permute-start.8) | collective-permute-done | bytes 32800 | tf_op jit(solution)/shard_map/ppermute | solution.py:403
  47.9 1.3 third.1
  49.2 1.3 collective-permute-start.11
  50.5 3.1 %collective-permute-start.12 = (bf16[64,320]{1,0:T(8,128)(2,1)S(1)}, bf16[64,320]{1,0:T(8,128)(2,1)S(1)}, u32[]{:S(2)}, u32[]{:S(2)}) collective-permute-start(bf16[64,320]{1,0:T(8,128)(2,1)S(1)} %get-tuple-element.42), channel_id=1, source_target_pairs={{24,0},{28,4},{16,8},{20,12},{8,16},{12,20},{0,24},{4,28},{25,1},{... | collective-permute-start | bytes 122888 | tf_op jit(solution)/shard_map/ppermute | solution.py:403
  54.0 2.5 %collective-permute-done.11 = bf16[64,320]{1,0:T(8,128)(2,1)S(1)} collective-permute-done((bf16[64,320]{1,0:T(8,128)(2,1)S(1)}, bf16[64,320]{1,0:T(8,128)(2,1)S(1)}, u32[]{:S(2)}, u32[]{:S(2)}) %collective-permute-start.11) | collective-permute-done | bytes 40992 | tf_op jit(solution)/shard_map/ppermute | solution.py:403
  56.6 1.6 collective-permute-start.13
  60.2 4.1 %collective-permute-done.13 = bf16[4,64,320]{2,1,0:T(8,128)(2,1)S(1)} collective-permute-done((bf16[4,64,320]{2,1,0:T(8,128)(2,1)S(1)}, bf16[4,64,320]{2,1,0:T(8,128)(2,1)S(1)}, u32[]{:S(2)}, u32[]{:S(2)}) %collective-permute-start.13) | collective-permute-done | bytes 163872 | tf_op jit(solution)/shard_map/ppermute | solution.py:403
  65.3 2.0 %collective-permute-done.15 = bf16[4,64,320]{2,1,0:T(8,128)(2,1)S(1)} collective-permute-done((bf16[4,64,320]{2,1,0:T(8,128)(2,1)S(1)}, bf16[4,64,320]{2,1,0:T(8,128)(2,1)S(1)}, u32[]{:S(2)}, u32[]{:S(2)}) %collective-permute-start.15) | collective-permute-done | bytes 163872 | tf_op jit(solution)/shard_map/ppermute | solution.py:415
  67.4 2.3 %collective-permute-done.16.far = bf16[16,64,320]{2,1,0:T(8,128)(2,1)S(1)} collective-permute-done((bf16[16,64,320]{2,1,0:T(8,128)(2,1)S(1)}, bf16[16,64,320]{2,1,0:T(8,128)(2,1)S(1)}, u32[]{:S(2)}, u32[]{:S(2)}) %collective-permute-start.16) | collective-permute-done | bytes 655392 | tf_op jit(solution)/shard_map/ppermute | solution.py:403
  69.7 9.5 %fourth.1 = (bf16[64,256]{1,0:T(8,128)(2,1)S(1)}, bf16[8,256,256]{2,1,0:T(8,128)(2,1)S(1)}, bf16[8,64,32]{2,1,0:T(8,128)(2,1)S(1)}) custom-call(s32[2]{0:T(128)S(1)} %pad_add_fusion.ids, bf16[16,64,320]{2,1,0:T(8,128)(2,1)S(1)} %constant_dynamic-update-slice_fusion.near, bf16[16,64,320]{2,1,0:T(8,128)(2,1)S(1)} %collective-permute-done.16.far, ...), custom_call_target="tpu_custom_call" | custom-call | flops 1000000000 | bytes 3866624 | tf_op jit(solution)/shard_map/fourth/pallas_call | solution.py:51
  79.3 3.5 %collective-permute-start.18 = (bf16[64,256]{1,0:T(8,128)(2,1)S(1)}, bf16[64,256]{1,0:T(8,128)(2,1)S(1)}, u32[]{:S(2)}, u32[]{:S(2)}) collective-permute-start(bf16[64,256]{1,0:T(8,128)(2,1)S(1)} %get-tuple-element.45), channel_id=1, source_target_pairs={{16,0},{20,4},{24,8},{28,12},{0,16},{4,20},{8,24},{12,28},{17,1},{... | collective-permute-start | bytes 98312 | tf_op jit(solution)/shard_map/ppermute | solution.py:403
  83.7 1.3 collective-permute-done.18
  84.9 3.6 %collective-permute-done.19 = bf16[64,256]{1,0:T(8,128)(2,1)S(1)} collective-permute-done((bf16[64,256]{1,0:T(8,128)(2,1)S(1)}, bf16[64,256]{1,0:T(8,128)(2,1)S(1)}, u32[]{:S(2)}, u32[]{:S(2)}) %collective-permute-start.19) | collective-permute-done | bytes 32800 | tf_op jit(solution)/shard_map/ppermute | solution.py:403
  88.6 1.6 collective-permute-start.20
  92.2 2.9 %collective-permute-done.20 = bf16[4,64,256]{2,1,0:T(8,128)(2,1)S(1)} collective-permute-done((bf16[4,64,256]{2,1,0:T(8,128)(2,1)S(1)}, bf16[4,64,256]{2,1,0:T(8,128)(2,1)S(1)}, u32[]{:S(2)}, u32[]{:S(2)}) %collective-permute-start.20) | collective-permute-done | bytes 131104 | tf_op jit(solution)/shard_map/ppermute | solution.py:403
  95.2 1.8 collective-permute-done.22
  97.2 1.4 collective-permute-start.25
  98.5 3.0 %collective-permute-start.26 = (bf16[64,256]{1,0:T(8,128)(2,1)S(1)}, bf16[64,256]{1,0:T(8,128)(2,1)S(1)}, u32[]{:S(2)}, u32[]{:S(2)}) collective-permute-start(bf16[64,256]{1,0:T(8,128)(2,1)S(1)} %get-tuple-element.50), channel_id=1, source_target_pairs={{24,0},{28,4},{16,8},{20,12},{8,16},{12,20},{0,24},{4,28},{25,1},{... | collective-permute-start | bytes 98312 | tf_op jit(solution)/shard_map/ppermute | solution.py:403
  102.1 2.1 %collective-permute-done.26 = bf16[64,256]{1,0:T(8,128)(2,1)S(1)} collective-permute-done((bf16[64,256]{1,0:T(8,128)(2,1)S(1)}, bf16[64,256]{1,0:T(8,128)(2,1)S(1)}, u32[]{:S(2)}, u32[]{:S(2)}) %collective-permute-start.26) | collective-permute-done | bytes 32800 | tf_op jit(solution)/shard_map/ppermute | solution.py:403
  105.5 3.8 %collective-permute-done.27.far = bf16[4,64,256]{2,1,0:T(8,128)(2,1)S(1)} collective-permute-done((bf16[4,64,256]{2,1,0:T(8,128)(2,1)S(1)}, bf16[4,64,256]{2,1,0:T(8,128)(2,1)S(1)}, u32[]{:S(2)}, u32[]{:S(2)}) %collective-permute-start.27) | collective-permute-done | bytes 131104 | tf_op jit(solution)/shard_map/ppermute | solution.py:403
  110.5 25.8 %second_weight.1 = bf16[1728,256]{1,0:T(8,128)(2,1)} custom-call(s32[2]{0:T(128)S(1)} %pad_add_fusion.ids, bf16[4,64,256]{2,1,0:T(8,128)(2,1)S(1)} %pad_maximum_fusion.3.near, bf16[4,64,256]{2,1,0:T(8,128)(2,1)S(1)} %collective-permute-done.27.far, bf16[8,96,256]{2,1,0:T(8,128)(2,1)S(1)} %copy-done.10, bf16[8,256,256]{2,1,0:T(8,128)(2,1)S(1)} %copy-done.8), custom_call_target="tpu_custom_call" | custom-call | flops 1000000000 | bytes 2588672 | tf_op jit(solution)/shard_map/second_weight/pallas_call | solution.py:51
  136.3 57.7 %last.1 = (bf16[64,128]{1,0:T(8,128)(2,1)}, bf16[1728,256]{1,0:T(8,128)(2,1)}) custom-call(s32[2]{0:T(128)S(1)} %pad_add_fusion.ids, bf16[16,64,256]{2,1,0:T(8,128)(2,1)S(1)} %constant_dynamic-update-slice_fusion.7.near, bf16[16,64,256]{2,1,0:T(8,128)(2,1)S(1)} %collective-permute-done.23.far, bf16[1728,256]{1,0:T(8,128)(2,1)S(1)} %bitcast.38, ...), custom_call_target="tpu_custom_call" | custom-call | flops 1000000000 | bytes 3752448 | tf_op jit(solution)/shard_map/last/pallas_call | solution.py:51
  (97 shorter events, 22.8 us)
Async XLA Ops:
  3.1 13.8 %copy-start.1 = (bf16[27,64,256]{2,1,0:T(8,128)(2,1)S(1)}, bf16[27,64,256]{2,1,0:T(8,128)(2,1)}, u32[]{:S(2)}) copy-start(bf16[27,64,256]{2,1,0:T(8,128)(2,1)} %param.15) | copy-start | bytes 2654212
  3.8 5.7 %collective-permute-start = (bf16[96,256]{1,0:T(8,128)(2,1)S(1)}, bf16[96,256]{1,0:T(8,128)(2,1)S(1)}, u32[]{:S(2)}, u32[]{:S(2)}) collective-permute-start(bf16[96,256]{1,0:T(8,128)(2,1)S(1)} %pack.1), channel_id=1, source_target_pairs={{8,0},{12,4},{0,8},{4,12},{24,16},{28,20},{16,24},{20,28},{9,1},{1... | collective-permute-start | bytes 147464 | tf_op jit(solution)/shard_map/ppermute | solution.py:403
  6.9 5.9 %collective-permute-start.1 = (bf16[96,256]{1,0:T(8,128)(2,1)S(1)}, bf16[96,256]{1,0:T(8,128)(2,1)S(1)}, u32[]{:S(2)}, u32[]{:S(2)}) collective-permute-start(bf16[96,256]{1,0:T(8,128)(2,1)S(1)} %pack.1), channel_id=1, source_target_pairs={{16,0},{20,4},{24,8},{28,12},{0,16},{4,20},{8,24},{12,28},{17,1},{... | collective-permute-start | bytes 147464 | tf_op jit(solution)/shard_map/ppermute | solution.py:403
  9.4 5.9 %collective-permute-start.2 = (bf16[96,256]{1,0:T(8,128)(2,1)S(1)}, bf16[96,256]{1,0:T(8,128)(2,1)S(1)}, u32[]{:S(2)}, u32[]{:S(2)}) collective-permute-start(bf16[96,256]{1,0:T(8,128)(2,1)S(1)} %pack.1), channel_id=1, source_target_pairs={{24,0},{28,4},{16,8},{20,12},{8,16},{12,20},{0,24},{4,28},{25,1},{... | collective-permute-start | bytes 147464 | tf_op jit(solution)/shard_map/ppermute | solution.py:403
  15.4 5.7 %collective-permute-start.3 = (bf16[4,96,256]{2,1,0:T(8,128)(2,1)S(1)}, bf16[4,96,256]{2,1,0:T(8,128)(2,1)S(1)}, u32[]{:S(2)}, u32[]{:S(2)}) collective-permute-start(bf16[4,96,256]{2,1,0:T(8,128)(2,1)S(1)} %pad_maximum_fusion.near), channel_id=1, source_target_pairs={{4,0},{0,4},{12,8},{8,12},{20,16},{16,20},{28,24},{24,28},{5,1},{1... | collective-permute-start | bytes 589832 | tf_op jit(solution)/shard_map/ppermute | solution.py:403
  17.6 16.6 %copy-start = (bf16[27,64,256]{2,1,0:T(8,128)(2,1)S(1)}, bf16[27,64,256]{2,1,0:T(8,128)(2,1)}, u32[]{:S(2)}) copy-start(bf16[27,64,256]{2,1,0:T(8,128)(2,1)} %param.16) | copy-start | bytes 2654212
  32.3 2.5 %collective-permute-start.4 = (bf16[64,384]{1,0:T(8,128)(2,1)S(1)}, bf16[64,384]{1,0:T(8,128)(2,1)S(1)}, u32[]{:S(2)}, u32[]{:S(2)}) collective-permute-start(bf16[64,384]{1,0:T(8,128)(2,1)S(1)} %get-tuple-element.29), channel_id=1, source_target_pairs={{1,0},{0,1},{3,2},{2,3},{5,4},{4,5},{7,6},{6,7},{9,8},{8,9},{11,10... | collective-permute-start | bytes 147464 | tf_op jit(solution)/shard_map/ppermute | solution.py:403
  32.3 4.2 %collective-permute-start.5 = (bf16[64,384]{1,0:T(8,128)(2,1)S(1)}, bf16[64,384]{1,0:T(8,128)(2,1)S(1)}, u32[]{:S(2)}, u32[]{:S(2)}) collective-permute-start(bf16[64,384]{1,0:T(8,128)(2,1)S(1)} %get-tuple-element.30), channel_id=1, source_target_pairs={{2,0},{3,1},{0,2},{1,3},{6,4},{7,5},{4,6},{5,7},{10,8},{11,9},{8,1... | collective-permute-start | bytes 147464 | tf_op jit(solution)/shard_map/ppermute | solution.py:403
  33.8 3.6 %collective-permute-start.6 = (bf16[64,384]{1,0:T(8,128)(2,1)S(1)}, bf16[64,384]{1,0:T(8,128)(2,1)S(1)}, u32[]{:S(2)}, u32[]{:S(2)}) collective-permute-start(bf16[64,384]{1,0:T(8,128)(2,1)S(1)} %get-tuple-element.31), channel_id=1, source_target_pairs={{3,0},{2,1},{1,2},{0,3},{7,4},{6,5},{5,6},{4,7},{11,8},{10,9},{9,1... | collective-permute-start | bytes 147464 | tf_op jit(solution)/shard_map/ppermute | solution.py:403
  42.9 1.9 collective-permute-start.7
  43.2 3.9 %collective-permute-start.8 = (bf16[64,256]{1,0:T(8,128)(2,1)S(1)}, bf16[64,256]{1,0:T(8,128)(2,1)S(1)}, u32[]{:S(2)}, u32[]{:S(2)}) collective-permute-start(bf16[64,256]{1,0:T(8,128)(2,1)S(1)} %get-tuple-element.35), channel_id=1, source_target_pairs={{2,0},{3,1},{0,2},{1,3},{6,4},{7,5},{4,6},{5,7},{10,8},{11,9},{8,1... | collective-permute-start | bytes 98312 | tf_op jit(solution)/shard_map/ppermute | solution.py:403
  44.4 3.6 %collective-permute-start.9 = (bf16[64,256]{1,0:T(8,128)(2,1)S(1)}, bf16[64,256]{1,0:T(8,128)(2,1)S(1)}, u32[]{:S(2)}, u32[]{:S(2)}) collective-permute-start(bf16[64,256]{1,0:T(8,128)(2,1)S(1)} %get-tuple-element.36), channel_id=1, source_target_pairs={{3,0},{2,1},{1,2},{0,3},{7,4},{6,5},{5,6},{4,7},{11,8},{10,9},{9,1... | collective-permute-start | bytes 98312 | tf_op jit(solution)/shard_map/ppermute | solution.py:403
  49.2 4.8 %collective-permute-start.10 = (bf16[64,320]{1,0:T(8,128)(2,1)S(1)}, bf16[64,320]{1,0:T(8,128)(2,1)S(1)}, u32[]{:S(2)}, u32[]{:S(2)}) collective-permute-start(bf16[64,320]{1,0:T(8,128)(2,1)S(1)} %get-tuple-element.40), channel_id=1, source_target_pairs={{8,0},{12,4},{0,8},{4,12},{24,16},{28,20},{16,24},{20,28},{9,1},{1... | collective-permute-start | bytes 122888 | tf_op jit(solution)/shard_map/ppermute | solution.py:403
  49.2 7.3 %collective-permute-start.11 = (bf16[64,320]{1,0:T(8,128)(2,1)S(1)}, bf16[64,320]{1,0:T(8,128)(2,1)S(1)}, u32[]{:S(2)}, u32[]{:S(2)}) collective-permute-start(bf16[64,320]{1,0:T(8,128)(2,1)S(1)} %get-tuple-element.41), channel_id=1, source_target_pairs={{16,0},{20,4},{24,8},{28,12},{0,16},{4,20},{8,24},{12,28},{17,1},{... | collective-permute-start | bytes 122888 | tf_op jit(solution)/shard_map/ppermute | solution.py:403
  50.5 6.0 %collective-permute-start.12 = (bf16[64,320]{1,0:T(8,128)(2,1)S(1)}, bf16[64,320]{1,0:T(8,128)(2,1)S(1)}, u32[]{:S(2)}, u32[]{:S(2)}) collective-permute-start(bf16[64,320]{1,0:T(8,128)(2,1)S(1)} %get-tuple-element.42), channel_id=1, source_target_pairs={{24,0},{28,4},{16,8},{20,12},{8,16},{12,20},{0,24},{4,28},{25,1},{... | collective-permute-start | bytes 122888 | tf_op jit(solution)/shard_map/ppermute | solution.py:403
  56.6 7.7 %collective-permute-start.13 = (bf16[4,64,320]{2,1,0:T(8,128)(2,1)S(1)}, bf16[4,64,320]{2,1,0:T(8,128)(2,1)S(1)}, u32[]{:S(2)}, u32[]{:S(2)}) collective-permute-start(bf16[4,64,320]{2,1,0:T(8,128)(2,1)S(1)} %pad_maximum_fusion.1), channel_id=1, source_target_pairs={{4,0},{0,4},{12,8},{8,12},{20,16},{16,20},{28,24},{24,28},{5,1},{1... | collective-permute-start | bytes 491528 | tf_op jit(solution)/shard_map/ppermute | solution.py:403
  58.1 7.1 %collective-permute-start.14 = (bf16[4,64,320]{2,1,0:T(8,128)(2,1)S(1)}, bf16[4,64,320]{2,1,0:T(8,128)(2,1)S(1)}, u32[]{:S(2)}, u32[]{:S(2)}) collective-permute-start(bf16[4,64,320]{2,1,0:T(8,128)(2,1)S(1)} %pad_maximum_fusion.1), channel_id=1, source_target_pairs={{2,0},{3,1},{0,2},{1,3},{6,4},{7,5},{4,6},{5,7},{10,8},{11,9},{8,1... | collective-permute-start | bytes 491528 | tf_op jit(solution)/shard_map/ppermute | solution.py:403
  59.1 8.2 %collective-permute-start.15 = (bf16[4,64,320]{2,1,0:T(8,128)(2,1)S(1)}, bf16[4,64,320]{2,1,0:T(8,128)(2,1)S(1)}, u32[]{:S(2)}, u32[]{:S(2)}) collective-permute-start(bf16[4,64,320]{2,1,0:T(8,128)(2,1)S(1)} %pad_maximum_fusion.1), channel_id=1, source_target_pairs={{6,0},{7,1},{4,2},{5,3},{2,4},{3,5},{0,6},{1,7},{14,8},{15,9},{12,... | collective-permute-start | bytes 491528 | tf_op jit(solution)/shard_map/ppermute | solution.py:415
  67.3 2.4 %collective-permute-start.16 = (bf16[16,64,320]{2,1,0:T(8,128)(2,1)S(1)}, bf16[16,64,320]{2,1,0:T(8,128)(2,1)S(1)}, u32[]{:S(2)}, u32[]{:S(2)}) collective-permute-start(bf16[16,64,320]{2,1,0:T(8,128)(2,1)S(1)} %constant_dynamic-update-slice_fusion.near), channel_id=1, source_target_pairs={{1,0},{0,1},{3,2},{2,3},{5,4},{4,5},{7,6},{6,7},{9,8},{8,9},{11,10... | collective-permute-start | bytes 1966088 | tf_op jit(solution)/shard_map/ppermute | solution.py:403
  79.2 25.1 %copy-start.7 = (bf16[8,256,256]{2,1,0:T(8,128)(2,1)}, bf16[8,256,256]{2,1,0:T(8,128)(2,1)S(1)}, u32[]{:S(2)}) copy-start(bf16[8,256,256]{2,1,0:T(8,128)(2,1)S(1)} %get-tuple-element.51.gall) | copy-start | bytes 3145732
  79.2 4.5 %collective-permute-start.17 = (bf16[64,256]{1,0:T(8,128)(2,1)S(1)}, bf16[64,256]{1,0:T(8,128)(2,1)S(1)}, u32[]{:S(2)}, u32[]{:S(2)}) collective-permute-start(bf16[64,256]{1,0:T(8,128)(2,1)S(1)} %get-tuple-element.45), channel_id=1, source_target_pairs={{8,0},{12,4},{0,8},{4,12},{24,16},{28,20},{16,24},{20,28},{9,1},{1... | collective-permute-start | bytes 98312 | tf_op jit(solution)/shard_map/ppermute | solution.py:403
  79.3 5.6 %collective-permute-start.18 = (bf16[64,256]{1,0:T(8,128)(2,1)S(1)}, bf16[64,256]{1,0:T(8,128)(2,1)S(1)}, u32[]{:S(2)}, u32[]{:S(2)}) collective-permute-start(bf16[64,256]{1,0:T(8,128)(2,1)S(1)} %get-tuple-element.45), channel_id=1, source_target_pairs={{16,0},{20,4},{24,8},{28,12},{0,16},{4,20},{8,24},{12,28},{17,1},{... | collective-permute-start | bytes 98312 | tf_op jit(solution)/shard_map/ppermute | solution.py:403
  82.9 5.7 %collective-permute-start.19 = (bf16[64,256]{1,0:T(8,128)(2,1)S(1)}, bf16[64,256]{1,0:T(8,128)(2,1)S(1)}, u32[]{:S(2)}, u32[]{:S(2)}) collective-permute-start(bf16[64,256]{1,0:T(8,128)(2,1)S(1)} %get-tuple-element.45), channel_id=1, source_target_pairs={{24,0},{28,4},{16,8},{20,12},{8,16},{12,20},{0,24},{4,28},{25,1},{... | collective-permute-start | bytes 98312 | tf_op jit(solution)/shard_map/ppermute | solution.py:403
  88.6 6.4 %collective-permute-start.20 = (bf16[4,64,256]{2,1,0:T(8,128)(2,1)S(1)}, bf16[4,64,256]{2,1,0:T(8,128)(2,1)S(1)}, u32[]{:S(2)}, u32[]{:S(2)}) collective-permute-start(bf16[4,64,256]{2,1,0:T(8,128)(2,1)S(1)} %pad_maximum_fusion.2), channel_id=1, source_target_pairs={{4,0},{0,4},{12,8},{8,12},{20,16},{16,20},{28,24},{24,28},{5,1},{1... | collective-permute-start | bytes 393224 | tf_op jit(solution)/shard_map/ppermute | solution.py:403
  90.2 5.0 %collective-permute-start.21 = (bf16[4,64,256]{2,1,0:T(8,128)(2,1)S(1)}, bf16[4,64,256]{2,1,0:T(8,128)(2,1)S(1)}, u32[]{:S(2)}, u32[]{:S(2)}) collective-permute-start(bf16[4,64,256]{2,1,0:T(8,128)(2,1)S(1)} %pad_maximum_fusion.2), channel_id=1, source_target_pairs={{2,0},{3,1},{0,2},{1,3},{6,4},{7,5},{4,6},{5,7},{10,8},{11,9},{8,1... | collective-permute-start | bytes 393224 | tf_op jit(solution)/shard_map/ppermute | solution.py:403
  91.1 5.9 %collective-permute-start.22 = (bf16[4,64,256]{2,1,0:T(8,128)(2,1)S(1)}, bf16[4,64,256]{2,1,0:T(8,128)(2,1)S(1)}, u32[]{:S(2)}, u32[]{:S(2)}) collective-permute-start(bf16[4,64,256]{2,1,0:T(8,128)(2,1)S(1)} %pad_maximum_fusion.2), channel_id=1, source_target_pairs={{6,0},{7,1},{4,2},{5,3},{2,4},{3,5},{0,6},{1,7},{14,8},{15,9},{12,... | collective-permute-start | bytes 393224 | tf_op jit(solution)/shard_map/ppermute | solution.py:415
  97.0 39.3 %collective-permute-start.23 = (bf16[16,64,256]{2,1,0:T(8,128)(2,1)S(1)}, bf16[16,64,256]{2,1,0:T(8,128)(2,1)S(1)}, u32[]{:S(2)}, u32[]{:S(2)}) collective-permute-start(bf16[16,64,256]{2,1,0:T(8,128)(2,1)S(1)} %constant_dynamic-update-slice_fusion.7.near), channel_id=1, source_target_pairs={{1,0},{0,1},{3,2},{2,3},{5,4},{4,5},{7,6},{6,7},{9,8},{8,9},{11,10... | collective-permute-start | bytes 1572872 | tf_op jit(solution)/shard_map/ppermute | solution.py:403
  97.1 4.5 %collective-permute-start.24 = (bf16[64,256]{1,0:T(8,128)(2,1)S(1)}, bf16[64,256]{1,0:T(8,128)(2,1)S(1)}, u32[]{:S(2)}, u32[]{:S(2)}) collective-permute-start(bf16[64,256]{1,0:T(8,128)(2,1)S(1)} %get-tuple-element.50), channel_id=1, source_target_pairs={{8,0},{12,4},{0,8},{4,12},{24,16},{28,20},{16,24},{20,28},{9,1},{1... | collective-permute-start | bytes 98312 | tf_op jit(solution)/shard_map/ppermute | solution.py:403
  97.2 5.0 %collective-permute-start.25 = (bf16[64,256]{1,0:T(8,128)(2,1)S(1)}, bf16[64,256]{1,0:T(8,128)(2,1)S(1)}, u32[]{:S(2)}, u32[]{:S(2)}) collective-permute-start(bf16[64,256]{1,0:T(8,128)(2,1)S(1)} %get-tuple-element.50), channel_id=1, source_target_pairs={{16,0},{20,4},{24,8},{28,12},{0,16},{4,20},{8,24},{12,28},{17,1},{... | collective-permute-start | bytes 98312 | tf_op jit(solution)/shard_map/ppermute | solution.py:403
  98.5 5.7 %collective-permute-start.26 = (bf16[64,256]{1,0:T(8,128)(2,1)S(1)}, bf16[64,256]{1,0:T(8,128)(2,1)S(1)}, u32[]{:S(2)}, u32[]{:S(2)}) collective-permute-start(bf16[64,256]{1,0:T(8,128)(2,1)S(1)} %get-tuple-element.50), channel_id=1, source_target_pairs={{24,0},{28,4},{16,8},{20,12},{8,16},{12,20},{0,24},{4,28},{25,1},{... | collective-permute-start | bytes 98312 | tf_op jit(solution)/shard_map/ppermute | solution.py:403
  104.3 5.0 %collective-permute-start.27 = (bf16[4,64,256]{2,1,0:T(8,128)(2,1)S(1)}, bf16[4,64,256]{2,1,0:T(8,128)(2,1)S(1)}, u32[]{:S(2)}, u32[]{:S(2)}) collective-permute-start(bf16[4,64,256]{2,1,0:T(8,128)(2,1)S(1)} %pad_maximum_fusion.3.near), channel_id=1, source_target_pairs={{4,0},{0,4},{12,8},{8,12},{20,16},{16,20},{28,24},{24,28},{5,1},{1... | collective-permute-start | bytes 393224 | tf_op jit(solution)/shard_map/ppermute | solution.py:403
  110.5 25.8 %copy-start.13 = (bf16[8,80,256]{2,1,0:T(8,128)(2,1)S(1)}, bf16[8,80,256]{2,1,0:T(8,128)(2,1)}, u32[]{:S(2)}) copy-start(bf16[8,80,256]{2,1,0:T(8,128)(2,1)} %copy-done.11) | copy-start | bytes 983044
  (15 other events, 42.5 us)

commit v2 on v1

--- a/solution.py
+++ b/solution.py
@@ -32,18 +32,13 @@
     return jnp.where(row == index_row, 1.0, 0.0).astype(BF)
 
 
-def loop(count, step, carry, group=3):
-    group = group if count % group == 0 else 1
-
-    def body(i, carry):
-        for j in range(group):
-            carry = step(i * group + j, carry)
-        return carry
-
-    return lax.fori_loop(0, count // group, body, carry)
-
-
-def call(kernel, outs, scratch, args, ids, flops=10**9, vmem=40, name=None):
+def loop(count, step, carry):
+    for i in range(count):
+        carry = step(i, carry)
+    return carry
+
+
+def call(kernel, outs, scratch, args, ids, flops=10**9, vmem=12, name=None):
     single = not isinstance(outs, (list, tuple))
     outs = [outs] if single else list(outs)
     moved = sum(a.size * a.dtype.itemsize for a in args)
@@ -82,17 +77,21 @@
         self.depth = self.koff * self.ch
 
 
-def pack_kernel(z, ids, feat, table, drop, out):
+def pack_kernel(z, ids, feat, owner, kmap, lists, drop, out, table):
     h, lanes = z.half, z.scan
     out[0:h, 0:lanes] = feat[0:h, :]
     out[0:h, lanes : 2 * lanes] = feat[h : 2 * h, :]
-    lend = hot(table[z.koff : z.koff + 1, lanes : lanes + z.hs], z.slots)
+    table[...] = jnp.full(table.shape, -1, jnp.int32)
+    table[0 : z.koff, :] = kmap[...] - z.shift
+    meta = slice(z.koff, z.koff + 1)
+    table[meta, 0:lanes] = owner[...]
+    table[meta, lanes + z.rim : lanes + 2 * z.rim] = lists[1:2, :]
+    table[meta, lanes + 2 * z.rim : lanes + 3 * z.rim] = lists[0:1, :]
+    lend = hot(table[meta, lanes : lanes + z.hs], z.slots)
     chosen = nn(drop[...].astype(F32).astype(BF), lend).astype(BF)
     out[h : 2 * h, 0 : z.hs] = chosen[0:h, :]
     out[h : 2 * h, z.hs : 2 * z.hs] = chosen[h : 2 * h, :]
-    row = lax.broadcasted_iota(jnp.int32, (z.kr, z.slots), 0)
-    value = table[...] - jnp.where(row < z.koff, z.shift, 0)
-    out[2 * h :, :] = value.astype(F32).astype(BF)
+    out[2 * h :, :] = table[...].astype(F32).astype(BF)
 
 
 def read_table(z, pay, brick):
@@ -125,7 +124,7 @@
         oh = hot(kmo[pl.ds(k, 1), :], z.slots)
         hh = hot(kmh[pl.ds(k, 1), :], z.hs)
         got = nn(table, oh) + nn(halo, hh)
-        dst[pl.ds(pl.multiple_of(k * z.ch, z.ch), z.ch), 0 : z.slots] = got.astype(BF)
+        dst[pl.ds(k * z.ch, z.ch), 0 : z.slots] = got.astype(BF)
         return carry
 
     loop(z.koff, step, 0)
@@ -198,7 +197,7 @@
         oh = hot(klo[pl.ds(k, 1), :], 2 * z.slots)
         hh = hot(klh[pl.ds(k, 1), :], 2 * z.hs)
         got = nn(pair, oh) + nn(pair_halo, hh)
-        rows = pl.ds(pl.multiple_of(k * z.ch, z.ch), z.ch)
+        rows = pl.ds(k * z.ch, z.ch)
         stack[rows, z.slots : z.slots + z.hs] = got.astype(BF)
         return carry
 
@@ -269,15 +268,11 @@
 
 
 def push(z, dst, weight, grad):
-    count = z.koff
-    size = z.depth // count
-
-    def step(i, carry):
-        rows = pl.ds(pl.multiple_of(i * size, size), size)
+    pieces = 3 if z.koff % 3 == 0 else z.koff
+    size = z.depth // pieces
+    for i in range(pieces):
+        rows = slice(i * size, (i + 1) * size)
         dst[rows, :] = nn(weight[rows, :], grad).astype(BF)
-        return carry
-
-    loop(count, step, 0)
 
 
 def fourth_kernel(z, ids, near, far, weight, pay, conv, keep, grad, gall, scan, pushed, kmo, kma, kmb):
@@ -300,7 +295,7 @@
 
     def step(k, carry):
         total, border = carry
-        rows = pl.ds(pl.multiple_of(k * z.ch, z.ch), z.ch)
+        rows = pl.ds(k * z.ch, z.ch)
         one = pl.ds(k, 1)
         total = total + nt(pushed[0, rows, :], hot(kmo[one, :], z.slots))
         border = border + nt(pushed[1, rows, :], hot(kmb[one, :], z.hs))
@@ -316,31 +311,19 @@
     grad[...] = (total * keep[:, 0 : z.slots] * slope_silu(conv[...])).astype(BF)
 
 
-def weight_sum(z, out, total, stack, kmo, kmh, table_at, halo_at, pay, gall):
-    factor = float(z.nb * z.slots) ** (-0.5)
-    pieces = 9 if z.koff % 9 == 0 else z.koff
-    size = z.depth // pieces
-
-    def brick(a, carry):
-        value = map_values(z, pay, a)
+def gather_kernel(z, first, count, ids, pay, table, halo, out, kmo, kmh):
+    def brick(i, carry):
+        value = map_values(z, pay, first + i)
         kmo[...] = own_index(z, value)
         kmh[...] = halo_index(z, value)
-        gather_own(z, stack, table_at(a), halo_at(a), kmo, kmh)
-        grads = gall[a]
-
-        def piece(i, carry):
-            rows = pl.ds(pl.multiple_of(i * size, size), size)
-            total[rows, :] = total[rows, :] + nt(stack[rows, :], grads)
-            return carry
-
-        return loop(pieces, piece, carry)
-
-    total[...] = jnp.zeros_like(total)
-    lax.fori_loop(0, z.nb, brick, 0)
-    out[...] = (total[...] * factor).astype(BF)
-
-
-def second_weight_kernel(z, ids, near, far, pay, gall, out, total, stack, kmo, kmh, table, lent, halo):
+        a = first + i
+        gather_own(z, out.at[i], table[a, 0 : z.ch, :], halo[a, 0 : z.ch, :], kmo, kmh)
+        return carry
+
+    lax.fori_loop(0, count, brick, 0)
+
+
+def table_kernel(z, ids, near, far, pay, table, halo, lent):
     b = ids[0]
     for q in range(z.nb):
         table[b ^ q] = (near if q % 2 == 0 else far)[q // 2]
@@ -349,14 +332,32 @@
         lent[a] = nn(table[a], lend).astype(BF)
     for a in range(z.nb):
         halo[a] = halo_of(z, lent, a)
-    weight_sum(z, out, total, stack, kmo, kmh, lambda a: table[a], lambda a: halo[a], pay, gall)
-
-
-def last_kernel(z, ids, near, far, weight, pay, vox, halo, scan, owner, out, wout, gall, pushed, total, stack, kmo, kmh):
+
+
+def weight_sum(z, out, stacks, gall):
+    factor = float(z.nb * z.slots) ** (-0.5)
+    pieces = 3 if z.koff % 3 == 0 else z.koff
+    size = z.depth // pieces
+    for i in range(pieces):
+        rows = slice(i * size, (i + 1) * size)
+        total = None
+        for n, stack in enumerate(stacks):
+            for j in range(stack.shape[0]):
+                part = nt(stack[j, rows, :], gall[n * stack.shape[0] + j])
+                total = part if total is None else total + part
+        out[rows, :] = (total * factor).astype(BF)
+
+
+def weight_kernel(z, ids, gall, *rest):
+    weight_sum(z, rest[-1], rest[:-1], gall)
+
+
+def last_kernel(z, ids, near, far, weight, pay, scan, *rest):
+    stacks, (out, wout, gall, pushed, kmo) = rest[:-5], rest[-5:]
     b = ids[0]
     collect(z, gall, ids, near, far)
-    mine = owner[...].astype(F32)
     row = read_table(z, pay, b)[z.koff : z.koff + 1, 0 : z.scan]
+    mine = jnp.transpose(jnp.broadcast_to(row, (8, z.scan)))[:, 0:1]
     square = (z.scan, z.scan)
     lane = lanes_of(square)
     sub = lax.broadcasted_iota(jnp.int32, square, 0)
@@ -376,7 +377,7 @@
         kmo[...] = map_values(z, pay, a)
 
         def step(k, got):
-            rows = pl.ds(pl.multiple_of(k * z.ch, z.ch), z.ch)
+            rows = pl.ds(k * z.ch, z.ch)
             chosen = jnp.where(wanted == kmo[pl.ds(k, 1), :], 1.0, 0.0).astype(BF)
             return got + nt(pushed[rows, :], chosen)
 
@@ -395,7 +396,7 @@
 
     result = lax.fori_loop(0, z.nb, brick, jnp.zeros((z.ch, z.scan), F32))
     out[...] = result.astype(BF)
-    weight_sum(z, wout, total, stack, kmo, kmh, lambda a: vox[a, 0 : z.ch, :], lambda a: halo[a, 0 : z.ch, :], pay, gall)
+    weight_sum(z, wout, stacks, gall)
 
 
 def swap(value, axis, mask):
@@ -453,11 +454,6 @@
     ids = jnp.stack([lax.axis_index("brick"), lax.axis_index("ch")]).astype(jnp.int32)
     sds = jax.ShapeDtypeStruct
     vm = pltpu.VMEM
-    pad = jnp.full((1, z.rim), -1, jnp.int32)
-    meta = jnp.concatenate([owner_map.reshape(1, z.scan), pad, send_lists[1:2], send_lists[0:1], pad], axis=1)
-    table = jnp.concatenate(
-        [kernel_map, meta, jnp.zeros((z.kr - z.koff - 1, z.slots), jnp.int32)], axis=0
-    )
     flat_first = weight_first.reshape(z.depth, z.all)
     flat_second = weight_second.reshape(z.depth, z.all)
     turned_first = flat_first.T
@@ -466,8 +462,8 @@
     payload = call(
         functools.partial(pack_kernel, z),
         sds((z.rows, z.slots), BF),
-        [],
-        [features, table, drop_first],
+        [vm((z.kr, z.slots), jnp.int32)],
+        [features, owner_map.reshape(1, z.scan), kernel_map, send_lists, drop_first],
         ids,
         name="pack",
     )
@@ -517,7 +513,33 @@
         ids,
         name="third",
     )
+    group = 2
+
+    def gathered(table, halo, name):
+        return [
+            call(
+                functools.partial(gather_kernel, z, i, group),
+                sds((group, z.depth, z.slots), BF),
+                ints,
+                [pay, table, halo],
+                ids,
+                flops=2 * 10**9,
+                name=name,
+            )
+            for i in range(0, nb, group)
+        ]
+
+    stacks_first = gathered(vox, halo, "gather_first")
     hidden_near, hidden_far = over_bricks(hidden, nb)
+    hidden_all, hidden_halo = call(
+        functools.partial(table_kernel, z),
+        [sds((nb, z.ch, z.slots), BF), sds((nb, z.ch, z.hs), BF)],
+        [vm((nb, z.ch, z.hs), BF)],
+        [hidden_near, hidden_far, pay],
+        ids,
+        name="table",
+    )
+    stacks_second = gathered(hidden_all, hidden_halo, "gather_second")
     near, far = over_all(sends, nb, nc)
     grad_first, gall, scan = call(
         functools.partial(fourth_kernel, z),
@@ -526,29 +548,18 @@
             sds((nb, z.all, z.slots), BF),
             sds((nb, z.ch, z.cap), BF),
         ],
-        [
-            vm((3, z.depth, z.slots), BF),
-            vm((z.kr, z.slots), jnp.int32),
-            vm((z.kr, z.slots), jnp.int32),
-            vm((z.kr, z.slots), jnp.int32),
-        ],
+        [vm((3, z.depth, z.slots), BF)] + [vm((z.kr, z.slots), jnp.int32)] * 3,
         [near, far, flat_second, pay, conv, keep],
         ids,
         name="fourth",
     )
     weight_grad_second = call(
-        functools.partial(second_weight_kernel, z),
+        functools.partial(weight_kernel, z),
         sds((z.depth, z.all), BF),
-        [
-            vm((z.depth, z.all), F32),
-            vm((z.depth, z.slots), BF),
-            *ints,
-            vm((nb, z.ch, z.slots), BF),
-            vm((nb, z.ch, z.hs), BF),
-            vm((nb, z.ch, z.hs), BF),
-        ],
-        [hidden_near, hidden_far, pay, gall],
+        [],
+        [gall, *stacks_second],
         ids,
+        flops=3 * 10**9,
         name="second_weight",
     )
     near, far = over_all([grad_first] * (nb // 2), nb, nc)
@@ -558,11 +569,9 @@
         [
             vm((nb, z.all, z.slots), BF),
             vm((z.depth, z.slots), BF),
-            vm((z.depth, z.all), F32),
-            vm((z.depth, z.slots), BF),
-            *ints,
+            vm((z.kr, z.slots), jnp.int32),
         ],
-        [near, far, flat_first, pay, vox, halo, scan, owner_map],
+        [near, far, flat_first, pay, scan, *stacks_first],
         ids,
         name="last",
     )

time: 194 us -> 118 us (0.61)
  Pallas kernels: 107 us -> 52 us
  waiting for transfers between devices: 43.6 us -> 25.4 us
  local copies, waits for them, and re-layouts: 9.6 us -> 5.91 us
    pallas_call x7 -> x16, Pallas kernels: 107 us -> 52 us  [call(): pl.pallas_call(kernel, out_shape=outs, in_specs=[pl.BlockSpec(memory_spac...]
    ppermute x26, waiting for transfers between devices: 39.8 us -> 21.2 us  [swap(): return lax.ppermute(value, axis, [(i ^ mask, i) for i in range(count)])]
    unnamed x51 -> x34, local copies, waits for them, and re-layouts: 6.77 us -> 3.81 us
  transfers between devices with their start and end apart: 28 -> 28, of which waited for: 21 -> 12; matrix products, arithmetic and copies ran while one was open for 1% -> 2% of each run, Pallas kernels for 13% -> 21%
where the time goes in v2:
time: 118 us
  Pallas kernels  52 us (44%)
  starting transfers between devices  33.3 us (28%)
  waiting for transfers between devices  25.4 us (22%)
  local copies, waits for them, and re-layouts  5.91 us (5%)
    pallas_call x16, Pallas kernels, call(): pl.pallas_call(kernel, out_shape=outs, in_specs=[pl.BlockSpec(memory_spac...  52 us
    ppermute x26, starting transfers between devices, swap(): return lax.ppermute(value, axis, [(i ^ mask, i) for i in range(count)])  32.3 us
    ppermute x26, waiting for transfers between devices, swap(): return lax.ppermute(value, axis, [(i ^ mask, i) for i in range(count)])  21.2 us
    ppermute x2, waiting for transfers between devices, swap_both(): return lax.ppermute(value, ('brick', 'ch'), pairs)  4.12 us
    unnamed x34, local copies, waits for them, and re-layouts  3.81 us
  transfers between devices with their start and end apart: 28, of which 12 were waited for; matrix products, arithmetic and copies ran while one was open for 2% of the time, Pallas kernels for 21%

profile of v2, /device:TPU:0, one launch (start us, length us, event | category | flops | bytes accessed | tf_op | source)
XLA Modules:
  0.0 117.7 jit_solution(15920155556850074592)
XLA Ops:
  5.1 5.1 %collective-permute-start.2 = (bf16[96,256]{1,0:T(8,128)(2,1)S(1)}, bf16[96,256]{1,0:T(8,128)(2,1)S(1)}, u32[]{:S(2)}, u32[]{:S(2)}) collective-permute-start(bf16[96,256]{1,0:T(8,128)(2,1)S(1)} %pack.1), channel_id=1, source_target_pairs={{24,0},{28,4},{16,8},{20,12},{8,16},{12,20},{0,24},{4,28},{25,1},{... | collective-permute-start | bytes 147464 | tf_op jit(solution)/shard_map/ppermute | solution.py:404
  12.3 2.9 %collective-permute-done.1 = bf16[96,256]{1,0:T(8,128)(2,1)S(1)} collective-permute-done((bf16[96,256]{1,0:T(8,128)(2,1)S(1)}, bf16[96,256]{1,0:T(8,128)(2,1)S(1)}, u32[]{:S(2)}, u32[]{:S(2)}) %collective-permute-start.1) | collective-permute-done | bytes 49184 | tf_op jit(solution)/shard_map/ppermute | solution.py:404
  15.2 1.6 %collective-permute-start.3 = (bf16[4,96,256]{2,1,0:T(8,128)(2,1)S(1)}, bf16[4,96,256]{2,1,0:T(8,128)(2,1)S(1)}, u32[]{:S(2)}, u32[]{:S(2)}) collective-permute-start(bf16[4,96,256]{2,1,0:T(8,128)(2,1)S(1)} %pad_maximum_fusion.near), channel_id=1, source_target_pairs={{4,0},{0,4},{12,8},{8,12},{20,16},{16,20},{28,24},{24,28},{5,1},{1... | collective-permute-start | bytes 589832 | tf_op jit(solution)/shard_map/ppermute | solution.py:404
  18.9 2.2 %collective-permute-done.3.far = bf16[4,96,256]{2,1,0:T(8,128)(2,1)S(1)} collective-permute-done((bf16[4,96,256]{2,1,0:T(8,128)(2,1)S(1)}, bf16[4,96,256]{2,1,0:T(8,128)(2,1)S(1)}, u32[]{:S(2)}, u32[]{:S(2)}) %collective-permute-start.3) | collective-permute-done | bytes 196640 | tf_op jit(solution)/shard_map/ppermute | solution.py:404
  21.0 5.3 %first.1 = (f32[64,384]{1,0:T(8,128)S(1)}, bf16[64,384]{1,0:T(8,128)(2,1)S(1)}, bf16[64,384]{1,0:T(8,128)(2,1)S(1)}, bf16[64,384]{1,0:T(8,128)(2,1)S(1)}, f32[64...) custom-call(s32[2]{0:T(128)S(1)} %pad_add_fusion.ids, ...), custom_call_target="tpu_custom_call" | custom-call | flops 1000000000 | bytes 2572288 | tf_op jit(solution)/shard_map/first/pallas_call | solution.py:46
  26.5 1.6 %collective-permute-start.5 = (bf16[64,384]{1,0:T(8,128)(2,1)S(1)}, bf16[64,384]{1,0:T(8,128)(2,1)S(1)}, u32[]{:S(2)}, u32[]{:S(2)}) collective-permute-start(bf16[64,384]{1,0:T(8,128)(2,1)S(1)} %get-tuple-element.32), channel_id=1, source_target_pairs={{2,0},{3,1},{0,2},{1,3},{6,4},{7,5},{4,6},{5,7},{10,8},{11,9},{8,1... | collective-permute-start | bytes 147464 | tf_op jit(solution)/shard_map/ppermute | solution.py:404
  28.3 2.3 %gather_first.4.rest_0_ = bf16[2,1728,256]{2,1,0:T(8,128)(2,1)S(1)} custom-call(s32[2]{0:T(128)S(1)} %pad_add_fusion.ids, bf16[8,96,256]{2,1,0:T(8,128)(2,1)S(1)} %get-tuple-element.45.pay, bf16[8,80,256]{2,1,0:T(8,128)(2,1)S(1)} %get-tuple-element.39.rest_4_.table, bf16[8,80,128]{2,1,0:T(8,128)(2,1)S(1)} %get-tuple-element.49.halo), custom_call_target="tpu_custom_call" | custom-call | flops 2000000000 | bytes 2654208 | tf_op jit(solution)/shard_map/gather_first/pallas_call | solution.py:46
  30.7 2.3 %gather_first.5.rest_1_ = bf16[2,1728,256]{2,1,0:T(8,128)(2,1)S(1)} custom-call(s32[2]{0:T(128)S(1)} %pad_add_fusion.ids, bf16[8,96,256]{2,1,0:T(8,128)(2,1)S(1)} %get-tuple-element.45.pay, bf16[8,80,256]{2,1,0:T(8,128)(2,1)S(1)} %get-tuple-element.39.rest_4_.table, bf16[8,80,128]{2,1,0:T(8,128)(2,1)S(1)} %get-tuple-element.49.halo), custom_call_target="tpu_custom_call" | custom-call | flops 2000000000 | bytes 2654208 | tf_op jit(solution)/shard_map/gather_first/pallas_call | solution.py:46
  33.1 2.5 %second.1 = (f32[64,256]{1,0:T(8,128)S(1)}, bf16[64,256]{1,0:T(8,128)(2,1)S(1)}, bf16[64,256]{1,0:T(8,128)(2,1)S(1)}, bf16[64,256]{1,0:T(8,128)(2,1)S(1)}, f32[6...) custom-call(s32[2]{0:T(128)S(1)} %pad_add_fusion.ids, f32[64,384]{1,0:T(8,128)S(1)} %get-tuple-element.30.rest_0_, ...), custom_call_target="tpu_custom_call" | custom-call | flops 1000000000 | bytes 1518592 | tf_op jit(solution)/shard_map/second/pallas_call | solution.py:46
  37.5 2.3 %gather_first.6.rest_2_ = bf16[2,1728,256]{2,1,0:T(8,128)(2,1)S(1)} custom-call(s32[2]{0:T(128)S(1)} %pad_add_fusion.ids, bf16[8,96,256]{2,1,0:T(8,128)(2,1)S(1)} %get-tuple-element.45.pay, bf16[8,80,256]{2,1,0:T(8,128)(2,1)S(1)} %get-tuple-element.39.rest_4_.table, bf16[8,80,128]{2,1,0:T(8,128)(2,1)S(1)} %get-tuple-element.49.halo), custom_call_target="tpu_custom_call" | custom-call | flops 2000000000 | bytes 2654208 | tf_op jit(solution)/shard_map/gather_first/pallas_call | solution.py:46
  39.9 2.1 %collective-permute-start.26 = (bf16[64,256]{1,0:T(8,128)(2,1)S(1)}, bf16[64,256]{1,0:T(8,128)(2,1)S(1)}, u32[]{:S(2)}, u32[]{:S(2)}) collective-permute-start(bf16[64,256]{1,0:T(8,128)(2,1)S(1)} %get-tuple-element.53), channel_id=1, source_target_pairs={{24,0},{28,4},{16,8},{20,12},{8,16},{12,20},{0,24},{4,28},{25,1},{... | collective-permute-start | bytes 98312 | tf_op jit(solution)/shard_map/ppermute | solution.py:404
  42.1 2.2 %collective-permute-start.24 = (bf16[64,256]{1,0:T(8,128)(2,1)S(1)}, bf16[64,256]{1,0:T(8,128)(2,1)S(1)}, u32[]{:S(2)}, u32[]{:S(2)}) collective-permute-start(bf16[64,256]{1,0:T(8,128)(2,1)S(1)} %get-tuple-element.53), channel_id=1, source_target_pairs={{8,0},{12,4},{0,8},{4,12},{24,16},{28,20},{16,24},{20,28},{9,1},{1... | collective-permute-start | bytes 98312 | tf_op jit(solution)/shard_map/ppermute | solution.py:404
  45.7 2.6 %collective-permute-start.11 = (bf16[64,320]{1,0:T(8,128)(2,1)S(1)}, bf16[64,320]{1,0:T(8,128)(2,1)S(1)}, u32[]{:S(2)}, u32[]{:S(2)}) collective-permute-start(bf16[64,320]{1,0:T(8,128)(2,1)S(1)} %get-tuple-element.43), channel_id=1, source_target_pairs={{16,0},{20,4},{24,8},{28,12},{0,16},{4,20},{8,24},{12,28},{17,1},{... | collective-permute-start | bytes 122888 | tf_op jit(solution)/shard_map/ppermute | solution.py:404
  48.2 1.8 %collective-permute-start.12 = (bf16[64,320]{1,0:T(8,128)(2,1)S(1)}, bf16[64,320]{1,0:T(8,128)(2,1)S(1)}, u32[]{:S(2)}, u32[]{:S(2)}) collective-permute-start(bf16[64,320]{1,0:T(8,128)(2,1)S(1)} %get-tuple-element.44), channel_id=1, source_target_pairs={{24,0},{28,4},{16,8},{20,12},{8,16},{12,20},{0,24},{4,28},{25,1},{... | collective-permute-start | bytes 122888 | tf_op jit(solution)/shard_map/ppermute | solution.py:404
  50.1 1.6 %collective-permute-start.27 = (bf16[4,64,256]{2,1,0:T(8,128)(2,1)S(1)}, bf16[4,64,256]{2,1,0:T(8,128)(2,1)S(1)}, u32[]{:S(2)}, u32[]{:S(2)}) collective-permute-start(bf16[4,64,256]{2,1,0:T(8,128)(2,1)S(1)} %pad_maximum_fusion.3.near), channel_id=1, source_target_pairs={{4,0},{0,4},{12,8},{8,12},{20,16},{16,20},{28,24},{24,28},{5,1},{1... | collective-permute-start | bytes 393224 | tf_op jit(solution)/shard_map/ppermute | solution.py:404
  51.6 2.4 %collective-permute-done.12 = bf16[64,320]{1,0:T(8,128)(2,1)S(1)} collective-permute-done((bf16[64,320]{1,0:T(8,128)(2,1)S(1)}, bf16[64,320]{1,0:T(8,128)(2,1)S(1)}, u32[]{:S(2)}, u32[]{:S(2)}) %collective-permute-start.12) | collective-permute-done | bytes 40992 | tf_op jit(solution)/shard_map/ppermute | solution.py:404
  54.1 1.6 %collective-permute-start.13 = (bf16[4,64,320]{2,1,0:T(8,128)(2,1)S(1)}, bf16[4,64,320]{2,1,0:T(8,128)(2,1)S(1)}, u32[]{:S(2)}, u32[]{:S(2)}) collective-permute-start(bf16[4,64,320]{2,1,0:T(8,128)(2,1)S(1)} %pad_maximum_fusion.1), channel_id=1, source_target_pairs={{4,0},{0,4},{12,8},{8,12},{20,16},{16,20},{28,24},{24,28},{5,1},{1... | collective-permute-start | bytes 491528 | tf_op jit(solution)/shard_map/ppermute | solution.py:404
  57.8 4.1 %collective-permute-done.13 = bf16[4,64,320]{2,1,0:T(8,128)(2,1)S(1)} collective-permute-done((bf16[4,64,320]{2,1,0:T(8,128)(2,1)S(1)}, bf16[4,64,320]{2,1,0:T(8,128)(2,1)S(1)}, u32[]{:S(2)}, u32[]{:S(2)}) %collective-permute-start.13) | collective-permute-done | bytes 163872 | tf_op jit(solution)/shard_map/ppermute | solution.py:404
  62.8 2.1 %collective-permute-done.15 = bf16[4,64,320]{2,1,0:T(8,128)(2,1)S(1)} collective-permute-done((bf16[4,64,320]{2,1,0:T(8,128)(2,1)S(1)}, bf16[4,64,320]{2,1,0:T(8,128)(2,1)S(1)}, u32[]{:S(2)}, u32[]{:S(2)}) %collective-permute-start.15) | collective-permute-done | bytes 163872 | tf_op jit(solution)/shard_map/ppermute | solution.py:416
  65.0 2.3 %gather_first.7.rest_3_ = bf16[2,1728,256]{2,1,0:T(8,128)(2,1)S(1)} custom-call(s32[2]{0:T(128)S(1)} %pad_add_fusion.ids, bf16[8,96,256]{2,1,0:T(8,128)(2,1)S(1)} %get-tuple-element.45.pay, bf16[8,80,256]{2,1,0:T(8,128)(2,1)S(1)} %get-tuple-element.39.rest_4_.table, bf16[8,80,128]{2,1,0:T(8,128)(2,1)S(1)} %get-tuple-element.49.halo), custom_call_target="tpu_custom_call" | custom-call | flops 2000000000 | bytes 2654208 | tf_op jit(solution)/shard_map/gather_first/pallas_call | solution.py:46
  68.2 2.5 %gather_second.4.rest_0_ = bf16[2,1728,256]{2,1,0:T(8,128)(2,1)S(1)} custom-call(s32[2]{0:T(128)S(1)} %pad_add_fusion.ids, bf16[8,96,256]{2,1,0:T(8,128)(2,1)S(1)} %get-tuple-element.45.pay, bf16[8,64,256]{2,1,0:T(8,128)(2,1)S(1)} %get-tuple-element.54.table, bf16[8,64,128]{2,1,0:T(8,128)(2,1)S(1)} %get-tuple-element.55.halo), custom_call_target="tpu_custom_call" | custom-call | flops 2000000000 | bytes 2555904 | tf_op jit(solution)/shard_map/gather_second/pallas_call | solution.py:46
  70.7 2.3 %gather_second.5.rest_1_ = bf16[2,1728,256]{2,1,0:T(8,128)(2,1)S(1)} custom-call(s32[2]{0:T(128)S(1)} %pad_add_fusion.ids, bf16[8,96,256]{2,1,0:T(8,128)(2,1)S(1)} %get-tuple-element.45.pay, bf16[8,64,256]{2,1,0:T(8,128)(2,1)S(1)} %get-tuple-element.54.table, bf16[8,64,128]{2,1,0:T(8,128)(2,1)S(1)} %get-tuple-element.55.halo), custom_call_target="tpu_custom_call" | custom-call | flops 2000000000 | bytes 2555904 | tf_op jit(solution)/shard_map/gather_second/pallas_call | solution.py:46
  73.1 4.7 %fourth.1 = (bf16[64,256]{1,0:T(8,128)(2,1)S(1)}, bf16[8,256,256]{2,1,0:T(8,128)(2,1)S(1)}, bf16[8,64,32]{2,1,0:T(8,128)(2,1)S(1)}) custom-call(s32[2]{0:T(128)S(1)} %pad_add_fusion.ids, bf16[16,64,320]{2,1,0:T(8,128)(2,1)S(1)} %constant_dynamic-update-slice_fusion.near, bf16[16,64,320]{2,1,0:T(8,128)(2,1)S(1)} %collective-permute-done.16.far, ...), custom_call_target="tpu_custom_call" | custom-call | flops 1000000000 | bytes 3866624 | tf_op jit(solution)/shard_map/fourth/pallas_call | solution.py:46
  77.9 2.6 %collective-permute-start.18 = (bf16[64,256]{1,0:T(8,128)(2,1)S(1)}, bf16[64,256]{1,0:T(8,128)(2,1)S(1)}, u32[]{:S(2)}, u32[]{:S(2)}) collective-permute-start(bf16[64,256]{1,0:T(8,128)(2,1)S(1)} %get-tuple-element.47), channel_id=1, source_target_pairs={{16,0},{20,4},{24,8},{28,12},{0,16},{4,20},{8,24},{12,28},{17,1},{... | collective-permute-start | bytes 98312 | tf_op jit(solution)/shard_map/ppermute | solution.py:404
  80.4 1.8 %collective-permute-start.19 = (bf16[64,256]{1,0:T(8,128)(2,1)S(1)}, bf16[64,256]{1,0:T(8,128)(2,1)S(1)}, u32[]{:S(2)}, u32[]{:S(2)}) collective-permute-start(bf16[64,256]{1,0:T(8,128)(2,1)S(1)} %get-tuple-element.47), channel_id=1, source_target_pairs={{24,0},{28,4},{16,8},{20,12},{8,16},{12,20},{0,24},{4,28},{25,1},{... | collective-permute-start | bytes 98312 | tf_op jit(solution)/shard_map/ppermute | solution.py:404
  82.8 3.4 %collective-permute-done.19 = bf16[64,256]{1,0:T(8,128)(2,1)S(1)} collective-permute-done((bf16[64,256]{1,0:T(8,128)(2,1)S(1)}, bf16[64,256]{1,0:T(8,128)(2,1)S(1)}, u32[]{:S(2)}, u32[]{:S(2)}) %collective-permute-start.19) | collective-permute-done | bytes 32800 | tf_op jit(solution)/shard_map/ppermute | solution.py:404
  89.8 2.1 %collective-permute-done.20 = bf16[4,64,256]{2,1,0:T(8,128)(2,1)S(1)} collective-permute-done((bf16[4,64,256]{2,1,0:T(8,128)(2,1)S(1)}, bf16[4,64,256]{2,1,0:T(8,128)(2,1)S(1)}, u32[]{:S(2)}, u32[]{:S(2)}) %collective-permute-start.20) | collective-permute-done | bytes 131104 | tf_op jit(solution)/shard_map/ppermute | solution.py:404
  93.1 2.0 %collective-permute-done.22 = bf16[4,64,256]{2,1,0:T(8,128)(2,1)S(1)} collective-permute-done((bf16[4,64,256]{2,1,0:T(8,128)(2,1)S(1)}, bf16[4,64,256]{2,1,0:T(8,128)(2,1)S(1)}, u32[]{:S(2)}, u32[]{:S(2)}) %collective-permute-start.22) | collective-permute-done | bytes 131104 | tf_op jit(solution)/shard_map/ppermute | solution.py:416
  95.2 2.3 %gather_second.6.rest_2_ = bf16[2,1728,256]{2,1,0:T(8,128)(2,1)S(1)} custom-call(s32[2]{0:T(128)S(1)} %pad_add_fusion.ids, bf16[8,96,256]{2,1,0:T(8,128)(2,1)S(1)} %get-tuple-element.45.pay, bf16[8,64,256]{2,1,0:T(8,128)(2,1)S(1)} %get-tuple-element.54.table, bf16[8,64,128]{2,1,0:T(8,128)(2,1)S(1)} %get-tuple-element.55.halo), custom_call_target="tpu_custom_call" | custom-call | flops 2000000000 | bytes 2555904 | tf_op jit(solution)/shard_map/gather_second/pallas_call | solution.py:46
  97.6 2.3 %gather_second.7.rest_3_ = bf16[2,1728,256]{2,1,0:T(8,128)(2,1)S(1)} custom-call(s32[2]{0:T(128)S(1)} %pad_add_fusion.ids, bf16[8,96,256]{2,1,0:T(8,128)(2,1)S(1)} %get-tuple-element.45.pay, bf16[8,64,256]{2,1,0:T(8,128)(2,1)S(1)} %get-tuple-element.54.table, bf16[8,64,128]{2,1,0:T(8,128)(2,1)S(1)} %get-tuple-element.55.halo), custom_call_target="tpu_custom_call" | custom-call | flops 2000000000 | bytes 2555904 | tf_op jit(solution)/shard_map/gather_second/pallas_call | solution.py:46
  99.9 3.5 %second_weight.1 = bf16[1728,256]{1,0:T(8,128)(2,1)} custom-call(s32[2]{0:T(128)S(1)} %pad_add_fusion.ids, bf16[8,256,256]{2,1,0:T(8,128)(2,1)S(1)} %get-tuple-element.52.gall, bf16[2,1728,256]{2,1,0:T(8,128)(2,1)S(1)} %gather_second.4.rest_0_, bf16[2,1728,256]{2,1,0:T(8,128)(2,1)S(1)} %gather_second.5.rest_1_, ...), custom_call_target="tpu_custom_call" | custom-call | flops 3000000000 | bytes 9011200 | tf_op jit(solution)/shard_map/second_weight/pallas_call | solution.py:46
  103.4 14.3 %last.1 = (bf16[64,128]{1,0:T(8,128)(2,1)}, bf16[1728,256]{1,0:T(8,128)(2,1)}) custom-call(s32[2]{0:T(128)S(1)} %pad_add_fusion.ids, bf16[16,64,256]{2,1,0:T(8,128)(2,1)S(1)} %constant_dynamic-update-slice_fusion.7.near, bf16[16,64,256]{2,1,0:T(8,128)(2,1)S(1)} %collective-permute-done.23.far, bf16[1728,256]{1,0:T(8,128)(2,1)S(1)} %bitcast.36, ...), custom_call_target="tpu_custom_call" | custom-call | flops 1000000000 | bytes 10338304 | tf_op jit(solution)/shard_map/last/pallas_call | solution.py:46
  (83 shorter events, 21.9 us)
Async XLA Ops:
  4.4 12.4 %copy-start = (bf16[27,64,256]{2,1,0:T(8,128)(2,1)S(1)}, bf16[27,64,256]{2,1,0:T(8,128)(2,1)}, u32[]{:S(2)}) copy-start(bf16[27,64,256]{2,1,0:T(8,128)(2,1)} %param.15) | copy-start | bytes 2654212
  5.1 7.2 %collective-permute-start.2 = (bf16[96,256]{1,0:T(8,128)(2,1)S(1)}, bf16[96,256]{1,0:T(8,128)(2,1)S(1)}, u32[]{:S(2)}, u32[]{:S(2)}) collective-permute-start(bf16[96,256]{1,0:T(8,128)(2,1)S(1)} %pack.1), channel_id=1, source_target_pairs={{24,0},{28,4},{16,8},{20,12},{8,16},{12,20},{0,24},{4,28},{25,1},{... | collective-permute-start | bytes 147464 | tf_op jit(solution)/shard_map/ppermute | solution.py:404
  10.2 5.0 %collective-permute-start.1 = (bf16[96,256]{1,0:T(8,128)(2,1)S(1)}, bf16[96,256]{1,0:T(8,128)(2,1)S(1)}, u32[]{:S(2)}, u32[]{:S(2)}) collective-permute-start(bf16[96,256]{1,0:T(8,128)(2,1)S(1)} %pack.1), channel_id=1, source_target_pairs={{16,0},{20,4},{24,8},{28,12},{0,16},{4,20},{8,24},{12,28},{17,1},{... | collective-permute-start | bytes 147464 | tf_op jit(solution)/shard_map/ppermute | solution.py:404
  10.2 5.0 %collective-permute-start = (bf16[96,256]{1,0:T(8,128)(2,1)S(1)}, bf16[96,256]{1,0:T(8,128)(2,1)S(1)}, u32[]{:S(2)}, u32[]{:S(2)}) collective-permute-start(bf16[96,256]{1,0:T(8,128)(2,1)S(1)} %pack.1), channel_id=1, source_target_pairs={{8,0},{12,4},{0,8},{4,12},{24,16},{28,20},{16,24},{20,28},{9,1},{1... | collective-permute-start | bytes 147464 | tf_op jit(solution)/shard_map/ppermute | solution.py:404
  15.2 5.8 %collective-permute-start.3 = (bf16[4,96,256]{2,1,0:T(8,128)(2,1)S(1)}, bf16[4,96,256]{2,1,0:T(8,128)(2,1)S(1)}, u32[]{:S(2)}, u32[]{:S(2)}) collective-permute-start(bf16[4,96,256]{2,1,0:T(8,128)(2,1)S(1)} %pad_maximum_fusion.near), channel_id=1, source_target_pairs={{4,0},{0,4},{12,8},{8,12},{20,16},{16,20},{28,24},{24,28},{5,1},{1... | collective-permute-start | bytes 589832 | tf_op jit(solution)/shard_map/ppermute | solution.py:404
  16.8 4.2 %copy-start.3 = (s32[64,256]{1,0:T(8,128)S(1)}, s32[64,256]{1,0:T(8,128)}, u32[]{:S(2)}) copy-start(s32[64,256]{1,0:T(8,128)} %drop.3) | copy-start | bytes 196612
  26.4 6.6 %collective-permute-start.4 = (bf16[64,384]{1,0:T(8,128)(2,1)S(1)}, bf16[64,384]{1,0:T(8,128)(2,1)S(1)}, u32[]{:S(2)}, u32[]{:S(2)}) collective-permute-start(bf16[64,384]{1,0:T(8,128)(2,1)S(1)} %get-tuple-element.31), channel_id=1, source_target_pairs={{1,0},{0,1},{3,2},{2,3},{5,4},{4,5},{7,6},{6,7},{9,8},{8,9},{11,10... | collective-permute-start | bytes 147464 | tf_op jit(solution)/shard_map/ppermute | solution.py:404
  26.5 6.6 %collective-permute-start.5 = (bf16[64,384]{1,0:T(8,128)(2,1)S(1)}, bf16[64,384]{1,0:T(8,128)(2,1)S(1)}, u32[]{:S(2)}, u32[]{:S(2)}) collective-permute-start(bf16[64,384]{1,0:T(8,128)(2,1)S(1)} %get-tuple-element.32), channel_id=1, source_target_pairs={{2,0},{3,1},{0,2},{1,3},{6,4},{7,5},{4,6},{5,7},{10,8},{11,9},{8,1... | collective-permute-start | bytes 147464 | tf_op jit(solution)/shard_map/ppermute | solution.py:404
  28.0 5.0 %collective-permute-start.6 = (bf16[64,384]{1,0:T(8,128)(2,1)S(1)}, bf16[64,384]{1,0:T(8,128)(2,1)S(1)}, u32[]{:S(2)}, u32[]{:S(2)}) collective-permute-start(bf16[64,384]{1,0:T(8,128)(2,1)S(1)} %get-tuple-element.33), channel_id=1, source_target_pairs={{3,0},{2,1},{1,2},{0,3},{7,4},{6,5},{5,6},{4,7},{11,8},{10,9},{9,1... | collective-permute-start | bytes 147464 | tf_op jit(solution)/shard_map/ppermute | solution.py:404
  35.6 6.5 %collective-permute-start.7 = (bf16[64,256]{1,0:T(8,128)(2,1)S(1)}, bf16[64,256]{1,0:T(8,128)(2,1)S(1)}, u32[]{:S(2)}, u32[]{:S(2)}) collective-permute-start(bf16[64,256]{1,0:T(8,128)(2,1)S(1)} %get-tuple-element.36), channel_id=1, source_target_pairs={{1,0},{0,1},{3,2},{2,3},{5,4},{4,5},{7,6},{6,7},{9,8},{8,9},{11,10... | collective-permute-start | bytes 98312 | tf_op jit(solution)/shard_map/ppermute | solution.py:404
  36.0 8.3 %collective-permute-start.8 = (bf16[64,256]{1,0:T(8,128)(2,1)S(1)}, bf16[64,256]{1,0:T(8,128)(2,1)S(1)}, u32[]{:S(2)}, u32[]{:S(2)}) collective-permute-start(bf16[64,256]{1,0:T(8,128)(2,1)S(1)} %get-tuple-element.37), channel_id=1, source_target_pairs={{2,0},{3,1},{0,2},{1,3},{6,4},{7,5},{4,6},{5,7},{10,8},{11,9},{8,1... | collective-permute-start | bytes 98312 | tf_op jit(solution)/shard_map/ppermute | solution.py:404
  37.5 6.8 %copy-start.4 = (s32[64,256]{1,0:T(8,128)S(1)}, s32[64,256]{1,0:T(8,128)}, u32[]{:S(2)}) copy-start(s32[64,256]{1,0:T(8,128)} %rest_5_.3) | copy-start | bytes 196612
  37.5 6.8 %copy-start.7 = (bf16[64,256]{1,0:T(8,128)(2,1)S(1)}, bf16[64,256]{1,0:T(8,128)(2,1)}, u32[]{:S(2)}) copy-start(bf16[64,256]{1,0:T(8,128)(2,1)} %rest_6_.1) | copy-start | bytes 98308
  37.5 6.8 %collective-permute-start.9 = (bf16[64,256]{1,0:T(8,128)(2,1)S(1)}, bf16[64,256]{1,0:T(8,128)(2,1)S(1)}, u32[]{:S(2)}, u32[]{:S(2)}) collective-permute-start(bf16[64,256]{1,0:T(8,128)(2,1)S(1)} %get-tuple-element.38), channel_id=1, source_target_pairs={{3,0},{2,1},{1,2},{0,3},{7,4},{6,5},{5,6},{4,7},{11,8},{10,9},{9,1... | collective-permute-start | bytes 98312 | tf_op jit(solution)/shard_map/ppermute | solution.py:404
  39.9 8.3 %collective-permute-start.26 = (bf16[64,256]{1,0:T(8,128)(2,1)S(1)}, bf16[64,256]{1,0:T(8,128)(2,1)S(1)}, u32[]{:S(2)}, u32[]{:S(2)}) collective-permute-start(bf16[64,256]{1,0:T(8,128)(2,1)S(1)} %get-tuple-element.53), channel_id=1, source_target_pairs={{24,0},{28,4},{16,8},{20,12},{8,16},{12,20},{0,24},{4,28},{25,1},{... | collective-permute-start | bytes 98312 | tf_op jit(solution)/shard_map/ppermute | solution.py:404
  42.0 8.1 %collective-permute-start.25 = (bf16[64,256]{1,0:T(8,128)(2,1)S(1)}, bf16[64,256]{1,0:T(8,128)(2,1)S(1)}, u32[]{:S(2)}, u32[]{:S(2)}) collective-permute-start(bf16[64,256]{1,0:T(8,128)(2,1)S(1)} %get-tuple-element.53), channel_id=1, source_target_pairs={{16,0},{20,4},{24,8},{28,12},{0,16},{4,20},{8,24},{12,28},{17,1},{... | collective-permute-start | bytes 98312 | tf_op jit(solution)/shard_map/ppermute | solution.py:404
  42.1 7.9 %collective-permute-start.24 = (bf16[64,256]{1,0:T(8,128)(2,1)S(1)}, bf16[64,256]{1,0:T(8,128)(2,1)S(1)}, u32[]{:S(2)}, u32[]{:S(2)}) collective-permute-start(bf16[64,256]{1,0:T(8,128)(2,1)S(1)} %get-tuple-element.53), channel_id=1, source_target_pairs={{8,0},{12,4},{0,8},{4,12},{24,16},{28,20},{16,24},{20,28},{9,1},{1... | collective-permute-start | bytes 98312 | tf_op jit(solution)/shard_map/ppermute | solution.py:404
  45.6 6.0 %collective-permute-start.10 = (bf16[64,320]{1,0:T(8,128)(2,1)S(1)}, bf16[64,320]{1,0:T(8,128)(2,1)S(1)}, u32[]{:S(2)}, u32[]{:S(2)}) collective-permute-start(bf16[64,320]{1,0:T(8,128)(2,1)S(1)} %get-tuple-element.42), channel_id=1, source_target_pairs={{8,0},{12,4},{0,8},{4,12},{24,16},{28,20},{16,24},{20,28},{9,1},{1... | collective-permute-start | bytes 122888 | tf_op jit(solution)/shard_map/ppermute | solution.py:404
  45.7 6.0 %collective-permute-start.11 = (bf16[64,320]{1,0:T(8,128)(2,1)S(1)}, bf16[64,320]{1,0:T(8,128)(2,1)S(1)}, u32[]{:S(2)}, u32[]{:S(2)}) collective-permute-start(bf16[64,320]{1,0:T(8,128)(2,1)S(1)} %get-tuple-element.43), channel_id=1, source_target_pairs={{16,0},{20,4},{24,8},{28,12},{0,16},{4,20},{8,24},{12,28},{17,1},{... | collective-permute-start | bytes 122888 | tf_op jit(solution)/shard_map/ppermute | solution.py:404
  48.2 5.9 %collective-permute-start.12 = (bf16[64,320]{1,0:T(8,128)(2,1)S(1)}, bf16[64,320]{1,0:T(8,128)(2,1)S(1)}, u32[]{:S(2)}, u32[]{:S(2)}) collective-permute-start(bf16[64,320]{1,0:T(8,128)(2,1)S(1)} %get-tuple-element.44), channel_id=1, source_target_pairs={{24,0},{28,4},{16,8},{20,12},{8,16},{12,20},{0,24},{4,28},{25,1},{... | collective-permute-start | bytes 122888 | tf_op jit(solution)/shard_map/ppermute | solution.py:404
  50.1 17.3 %collective-permute-start.27 = (bf16[4,64,256]{2,1,0:T(8,128)(2,1)S(1)}, bf16[4,64,256]{2,1,0:T(8,128)(2,1)S(1)}, u32[]{:S(2)}, u32[]{:S(2)}) collective-permute-start(bf16[4,64,256]{2,1,0:T(8,128)(2,1)S(1)} %pad_maximum_fusion.3.near), channel_id=1, source_target_pairs={{4,0},{0,4},{12,8},{8,12},{20,16},{16,20},{28,24},{24,28},{5,1},{1... | collective-permute-start | bytes 393224 | tf_op jit(solution)/shard_map/ppermute | solution.py:404
  54.1 7.7 %collective-permute-start.13 = (bf16[4,64,320]{2,1,0:T(8,128)(2,1)S(1)}, bf16[4,64,320]{2,1,0:T(8,128)(2,1)S(1)}, u32[]{:S(2)}, u32[]{:S(2)}) collective-permute-start(bf16[4,64,320]{2,1,0:T(8,128)(2,1)S(1)} %pad_maximum_fusion.1), channel_id=1, source_target_pairs={{4,0},{0,4},{12,8},{8,12},{20,16},{16,20},{28,24},{24,28},{5,1},{1... | collective-permute-start | bytes 491528 | tf_op jit(solution)/shard_map/ppermute | solution.py:404
  55.7 7.1 %collective-permute-start.14 = (bf16[4,64,320]{2,1,0:T(8,128)(2,1)S(1)}, bf16[4,64,320]{2,1,0:T(8,128)(2,1)S(1)}, u32[]{:S(2)}, u32[]{:S(2)}) collective-permute-start(bf16[4,64,320]{2,1,0:T(8,128)(2,1)S(1)} %pad_maximum_fusion.1), channel_id=1, source_target_pairs={{2,0},{3,1},{0,2},{1,3},{6,4},{7,5},{4,6},{5,7},{10,8},{11,9},{8,1... | collective-permute-start | bytes 491528 | tf_op jit(solution)/shard_map/ppermute | solution.py:404
  57.2 7.7 %collective-permute-start.15 = (bf16[4,64,320]{2,1,0:T(8,128)(2,1)S(1)}, bf16[4,64,320]{2,1,0:T(8,128)(2,1)S(1)}, u32[]{:S(2)}, u32[]{:S(2)}) collective-permute-start(bf16[4,64,320]{2,1,0:T(8,128)(2,1)S(1)} %pad_maximum_fusion.1), channel_id=1, source_target_pairs={{6,0},{7,1},{4,2},{5,3},{2,4},{3,5},{0,6},{1,7},{14,8},{15,9},{12,... | collective-permute-start | bytes 491528 | tf_op jit(solution)/shard_map/ppermute | solution.py:416
  64.9 8.1 %collective-permute-start.16 = (bf16[16,64,320]{2,1,0:T(8,128)(2,1)S(1)}, bf16[16,64,320]{2,1,0:T(8,128)(2,1)S(1)}, u32[]{:S(2)}, u32[]{:S(2)}) collective-permute-start(bf16[16,64,320]{2,1,0:T(8,128)(2,1)S(1)} %constant_dynamic-update-slice_fusion.near), channel_id=1, source_target_pairs={{1,0},{0,1},{3,2},{2,3},{5,4},{4,5},{7,6},{6,7},{9,8},{8,9},{11,10... | collective-permute-start | bytes 1966088 | tf_op jit(solution)/shard_map/ppermute | solution.py:404
  77.8 4.5 %collective-permute-start.17 = (bf16[64,256]{1,0:T(8,128)(2,1)S(1)}, bf16[64,256]{1,0:T(8,128)(2,1)S(1)}, u32[]{:S(2)}, u32[]{:S(2)}) collective-permute-start(bf16[64,256]{1,0:T(8,128)(2,1)S(1)} %get-tuple-element.47), channel_id=1, source_target_pairs={{8,0},{12,4},{0,8},{4,12},{24,16},{28,20},{16,24},{20,28},{9,1},{1... | collective-permute-start | bytes 98312 | tf_op jit(solution)/shard_map/ppermute | solution.py:404
  77.9 4.9 %collective-permute-start.18 = (bf16[64,256]{1,0:T(8,128)(2,1)S(1)}, bf16[64,256]{1,0:T(8,128)(2,1)S(1)}, u32[]{:S(2)}, u32[]{:S(2)}) collective-permute-start(bf16[64,256]{1,0:T(8,128)(2,1)S(1)} %get-tuple-element.47), channel_id=1, source_target_pairs={{16,0},{20,4},{24,8},{28,12},{0,16},{4,20},{8,24},{12,28},{17,1},{... | collective-permute-start | bytes 98312 | tf_op jit(solution)/shard_map/ppermute | solution.py:404
  80.4 5.7 %collective-permute-start.19 = (bf16[64,256]{1,0:T(8,128)(2,1)S(1)}, bf16[64,256]{1,0:T(8,128)(2,1)S(1)}, u32[]{:S(2)}, u32[]{:S(2)}) collective-permute-start(bf16[64,256]{1,0:T(8,128)(2,1)S(1)} %get-tuple-element.47), channel_id=1, source_target_pairs={{24,0},{28,4},{16,8},{20,12},{8,16},{12,20},{0,24},{4,28},{25,1},{... | collective-permute-start | bytes 98312 | tf_op jit(solution)/shard_map/ppermute | solution.py:404
  86.2 5.7 %collective-permute-start.20 = (bf16[4,64,256]{2,1,0:T(8,128)(2,1)S(1)}, bf16[4,64,256]{2,1,0:T(8,128)(2,1)S(1)}, u32[]{:S(2)}, u32[]{:S(2)}) collective-permute-start(bf16[4,64,256]{2,1,0:T(8,128)(2,1)S(1)} %pad_maximum_fusion.2), channel_id=1, source_target_pairs={{4,0},{0,4},{12,8},{8,12},{20,16},{16,20},{28,24},{24,28},{5,1},{1... | collective-permute-start | bytes 393224 | tf_op jit(solution)/shard_map/ppermute | solution.py:404
  87.7 5.4 %collective-permute-start.21 = (bf16[4,64,256]{2,1,0:T(8,128)(2,1)S(1)}, bf16[4,64,256]{2,1,0:T(8,128)(2,1)S(1)}, u32[]{:S(2)}, u32[]{:S(2)}) collective-permute-start(bf16[4,64,256]{2,1,0:T(8,128)(2,1)S(1)} %pad_maximum_fusion.2), channel_id=1, source_target_pairs={{2,0},{3,1},{0,2},{1,3},{6,4},{7,5},{4,6},{5,7},{10,8},{11,9},{8,1... | collective-permute-start | bytes 393224 | tf_op jit(solution)/shard_map/ppermute | solution.py:404
  89.2 5.9 %collective-permute-start.22 = (bf16[4,64,256]{2,1,0:T(8,128)(2,1)S(1)}, bf16[4,64,256]{2,1,0:T(8,128)(2,1)S(1)}, u32[]{:S(2)}, u32[]{:S(2)}) collective-permute-start(bf16[4,64,256]{2,1,0:T(8,128)(2,1)S(1)} %pad_maximum_fusion.2), channel_id=1, source_target_pairs={{6,0},{7,1},{4,2},{5,3},{2,4},{3,5},{0,6},{1,7},{14,8},{15,9},{12,... | collective-permute-start | bytes 393224 | tf_op jit(solution)/shard_map/ppermute | solution.py:416
  95.2 8.3 %collective-permute-start.23 = (bf16[16,64,256]{2,1,0:T(8,128)(2,1)S(1)}, bf16[16,64,256]{2,1,0:T(8,128)(2,1)S(1)}, u32[]{:S(2)}, u32[]{:S(2)}) collective-permute-start(bf16[16,64,256]{2,1,0:T(8,128)(2,1)S(1)} %constant_dynamic-update-slice_fusion.7.near), channel_id=1, source_target_pairs={{1,0},{0,1},{3,2},{2,3},{5,4},{4,5},{7,6},{6,7},{9,8},{8,9},{11,10... | collective-permute-start | bytes 1572872 | tf_op jit(solution)/shard_map/ppermute | solution.py:404
  (7 other events, 8.4 us)
